TPU v7x, 32 devices: a whole 2x2x4 slice. The times are simulated.
32 devices in a mesh: mic: 8 (over z, x), orient: 4 (over y, core).
Axes of the slice: x: 2, y: 2, z: 4, core: 2. Of those that a mesh axis runs over, the one named last changes fastest.
Arguments:
- micrograph: bfloat16 [3072, 384], P('mic'), may hold values from -6 to 6
- search_spectra: bfloat16 [64, 384, 768], P('orient', 'mic'), may hold values from -6 to 6
- refine_spectra: bfloat16 [8, 32, 384, 768], P('mic', 'orient'), may hold values from -6 to 6
- ctf: float32 [384, 384], replicated, may hold values from -1 to 1
- ref_owner: int32 [128, 1], P(('mic', 'orient')), may hold values from 0 to 3; in each aligned block of 4 rows (0 to 3, 4 to 7, ...) at most 2 rows name the same one
- ref_slot: int32 [128, 1], P(('mic', 'orient')), may hold values from 0 to 7
Outputs:
- peak_map: float32 [3072, 384], P('mic')
- mean_map: float32 [3072, 384], P('mic')
- scaled_peak: float32 [3072, 384], P('mic')
- refined_map: float32 [3072, 384], P('mic')
Inputs may be any that keep to these rules, and one draw needn't show every extreme that they name: `ref_owner`: in each aligned block of 4 rows (the list entries of one micrograph that one orientation block handles) no owner is named more than 2 times, and in some blocks one owner is named exactly 2 times.
All inputs are finite; a program needn't handle non-finite values.
Results may differ from a plain program's by a relative error of at most 0.0086.
Values may be sent and summed in bfloat16 or wider, within the bound.
A program may use at most 128 MiB of HBM per device.

v0:
```python
import math

import jax
import jax.numpy as jnp
from jax import lax
from jax.sharding import PartitionSpec as P


def merged_2(value, axis, join):
    gathered = jax.tree.map(
        lambda a, kind: lax.all_gather(a.astype(kind), axis),
        value,
        (jnp.bfloat16, jnp.bfloat16, jnp.bfloat16, jnp.bfloat16),
    )

    def take(source):
        return jax.tree.map(
            lambda a, own: lax.dynamic_index_in_dim(a, source, 0, False).astype(own.dtype),
            gathered,
            value,
        )

    return lax.fori_loop(
        1, lax.axis_size(axis), lambda source, state: join(state, take(source)), take(0)
    )


def make_tables(box_edge):
    positions = jnp.arange(box_edge, dtype=jnp.int32)
    products = positions[:, None] * positions[None, :] % box_edge
    angles = products.astype(jnp.float32) * (2.0 * math.pi / box_edge)
    cosine = jnp.cos(angles)
    sines = jnp.sin(angles)
    fwd_cos = cosine.astype(jnp.bfloat16)
    fwd_sin = sines.astype(jnp.bfloat16)
    inv_cos = (cosine / box_edge).astype(jnp.bfloat16)
    inv_sin = (sines / box_edge).astype(jnp.bfloat16)
    fwd_half = jnp.concatenate([fwd_cos, -fwd_sin], axis=1)
    fwd_full = jnp.stack([jnp.stack([fwd_cos, fwd_sin], -1), jnp.stack([-fwd_sin, fwd_cos], -1)], 0)
    inv_cols = jnp.concatenate(
        [jnp.concatenate([inv_cos, inv_sin], 1), jnp.concatenate([-inv_sin, inv_cos], 1)], 0
    )
    inv_rows = jnp.stack([inv_cos, -inv_sin], -1)
    return (fwd_half, fwd_full, inv_cols, inv_rows)


def forward(tile_image, fwd_half, fwd_full):
    box_edge = tile_image.shape[0]
    half_spectrum = jnp.dot(tile_image, fwd_half, preferred_element_type=jnp.float32).astype(
        jnp.bfloat16
    )
    stacked = half_spectrum.reshape(box_edge, 2, box_edge)
    spectrum = jnp.einsum("dykc,kcx->ydx", fwd_full, stacked, preferred_element_type=jnp.float32)
    return spectrum.reshape(box_edge, 2 * box_edge).astype(jnp.bfloat16)


def multiply(spectrum, filtered):
    box_edge = spectrum.shape[-1] // 2
    spec_real = spectrum[..., :box_edge].astype(jnp.float32)
    spec_imag = spectrum[..., box_edge:].astype(jnp.float32)
    filt_real = filtered[..., :box_edge].astype(jnp.float32)
    filt_imag = filtered[..., box_edge:].astype(jnp.float32)
    prod_real = spec_real * filt_real + spec_imag * filt_imag
    prod_imag = spec_imag * filt_real - spec_real * filt_imag
    return jnp.concatenate([prod_real, prod_imag], -1).astype(jnp.bfloat16)


def column_pass(product, inv_cols):
    return jnp.einsum("trl,lm->trm", product, inv_cols, preferred_element_type=jnp.float32).astype(
        jnp.bfloat16
    )


def row_pass(halfway, inv_rows):
    box_edge = halfway.shape[1]
    stacked = halfway.reshape(halfway.shape[0], box_edge, 2, box_edge)
    return jnp.einsum("ykc,tkcx->tyx", inv_rows, stacked, preferred_element_type=jnp.float32)


def combine(left, right):
    return (
        jnp.maximum(left[0], right[0]),
        left[1] + right[1],
        left[2] + right[2],
        jnp.maximum(left[3], right[3]),
    )


def body(micrograph, search_spectra, refine_spectra, ctf, ref_owner, ref_slot):
    box_edge = micrograph.shape[1]
    fwd_half, fwd_full, inv_cols, inv_rows = make_tables(box_edge)
    ctf_gain = jnp.concatenate([ctf, ctf], 1)
    rows_owned = search_spectra.shape[1]
    first_row = lax.axis_index("mic") * rows_owned
    own_gain = lax.dynamic_slice_in_dim(ctf_gain, first_row, rows_owned, 0)
    search_filtered = (search_spectra.astype(jnp.float32) * own_gain).astype(jnp.bfloat16)
    spectrum = forward(micrograph, fwd_half, fwd_full)
    halfway = column_pass(
        multiply(spectrum, lax.all_gather(search_filtered, "mic", axis=1, tiled=True)), inv_cols
    )
    correlations = row_pass(halfway, inv_rows)
    peak_local = jnp.max(correlations, axis=0)
    total_local = jnp.sum(correlations, axis=0)
    square_local = jnp.sum(correlations * correlations, axis=0)
    library = refine_spectra[0]
    library_filtered = (library.astype(jnp.float32) * ctf_gain).astype(jnp.bfloat16)
    block_size = library.shape[0]
    owners = ref_owner[:, 0]
    slot_ids = ref_slot[:, 0]
    gathered = lax.all_gather(library_filtered, "orient", axis=0, tiled=True)
    picked = jnp.take(gathered, owners * block_size + slot_ids, axis=0)
    picked_product = multiply(spectrum, picked)
    refined_local = jnp.max(row_pass(column_pass(picked_product, inv_cols), inv_rows), axis=0)
    merged = merged_2((peak_local, total_local, square_local, refined_local), "orient", combine)
    peak_map, total_map, square_map, refined_map = merged
    count = float(lax.axis_size("orient") * search_spectra.shape[0])
    mean_map = total_map / count
    scaled_peak = peak_map * lax.rsqrt(square_map / count + 1e-05)
    return (peak_map, mean_map, scaled_peak, refined_map)


def solution(mesh):
    in_specs = (
        P("mic", None),
        P("orient", "mic", None),
        P("mic", "orient", None, None),
        P(),
        P(("mic", "orient"), None),
        P(("mic", "orient"), None),
    )
    out_specs = (P("mic", None), P("mic", None), P("mic", None), P("mic", None))
    return jax.shard_map(body, mesh=mesh, in_specs=in_specs, out_specs=out_specs, check_vma=False)
```

profile of v0, /device:TPU:0, one launch (start us, length us, event | category | flops | bytes accessed | tf_op | source)
XLA Modules:
  0.0 369.3 jit_solution(18141209216676952182)
XLA Ops:
  9.6 1.3 multiply_convert_fusion
  11.0 5.3 %fusion.8 = bf16[8,384,768]{2,1,0:T(8,128)(2,1)} fusion(bf16[1,8,384,768]{3,2,1,0:T(8,128)(2,1)} %param.10, f32[384,768]{1,0:T(8,128)S(1)} %constant_dynamic-update-slice_fusion), kind=kLoop, calls=%fused_computation.18 | loop fusion | flops 7077888 | bytes 10616832 | tf_op jit(solution)/shard_map/convert_element_type | solution.py:106
  16.4 2.3 fusion.52
  18.7 2.3 fusion.45
  21.0 2.3 fusion.51
  23.4 2.5 fusion.39
  27.9 2.3 fusion.53
  30.2 2.3 fusion.50
  32.5 2.3 multiply_convert_fusion.2
  34.9 2.6 multiply_convert_fusion.3
  37.5 114.4 %all-gather.11.cloned.1.call-done = bf16[16,384,768]{2,1,0:T(8,128)(2,1)} async-done(((bf16[16,48,768]{2,1,0:T(8,128)(2,1)}), bf16[16,384,768]{2,1,0:T(8,128)(2,1)}) %all-gather.11.cloned.1.call-update) | async-done | bytes 9437200 | tf_op jit(solution)/shard_map/all_gather | solution.py:99
  151.8 5.9 %fusion.1 = (bf16[16,384,384]{2,1,0:T(8,128)(2,1)S(1)}, bf16[16,384,384]{2,1,0:T(8,128)(2,1)S(1)}) fusion(f32[384,384]{1,0:T(8,128)S(1)} %copy.17, f32[384,384]{1,0:T(8,128)S(1)} %copy.16, bf16[16,384,768]{2,1,0:T(8,128)(2,1)} %all-gather.11.cloned.1.call-done), kind=kLoop, calls=%fused_computation.10 | loop fusion | flops 23592960 | bytes 20054016 | tf_op jit(solution)/shard_map/convert.11
  157.8 10.3 %fusion.10 = bf16[16,384,768]{2,1,0:T(8,128)(2,1)} fusion(bf16[16,384,384]{2,1,0:T(8,128)(2,1)S(1)} %get-tuple-element.268, bf16[16,384,384]{2,1,0:T(8,128)(2,1)S(1)} %get-tuple-element.267, bf16[384,384]{1,0:T(8,128)(2,1)S(1)} %get-tuple-element.278, bf16[384,384]{1,0:T(8,128)(2,1)S(1)} %fusion.53, bf16[384,384]{1,0:T(8,128)(2,1)S(1)} %get-tuple-element.277), kind=kOutput, calls=%fused_computation.23 | convolution fusion | flops 7276068864 | bytes 19759104 | tf_op jit(solution)/shard_map/trl,lm->trm/dot_general | solution.py:69
  168.0 12.8 %copy.33 = bf16[16,384,768]{1,2,0:T(8,128)(2,1)} copy(bf16[16,384,768]{2,1,0:T(8,128)(2,1)} %fusion.10) | data formatting | bytes 18874368 | tf_op jit(solution)/shard_map/reshape | solution.py:76
  180.9 11.6 %fusion.9 = (bf16[384,384]{0,1:T(8,128)(2,1)}, bf16[384,384]{0,1:T(8,128)(2,1)}, bf16[384,384]{0,1:T(8,128)(2,1)}) fusion(bf16[16,384,2,384]{1,3,2,0:T(8,128)(2,1)} %bitcast.74, bf16[384,384,1]{1,0,2:T(8,128)(2,1)S(1)} %fusion.50, bf16[384,384,1]{1,0,2:T(8,128)(2,1)S(1)} %multiply_convert_fusion.2), kind=kOutput, calls=%fused_computation.22 | convolution fusion | flops 3633168384 | bytes 10911744 | tf_op jit(solution)/shard_map/ykc,tkcx->tyx/dot_general | solution.py:77
  193.8 77.9 %all-gather.13.cloned.1.call-done = bf16[32,384,768]{2,1,0:T(8,128)(2,1)} async-done(((bf16[8,384,768]{2,1,0:T(8,128)(2,1)}), bf16[32,384,768]{2,1,0:T(8,128)(2,1)}) %all-gather.13.cloned.1.call-update) | async-done | bytes 18874384 | tf_op jit(solution)/shard_map/all_gather | solution.py:110
  271.6 7.1 %gather_fusion = bf16[4,384,768]{2,1,0:T(8,128)(2,1)S(1)} fusion(bf16[32,384,768]{2,1,0:T(8,128)(2,1)} %all-gather.13.cloned.1.call-done, s32[1024]{0:T(1024)S(1)} %pad_clamp_fusion), kind=kCustom, calls=%fused_computation | custom fusion | bytes 4718608 | tf_op jit(solution)/shard_map/jit(_take)/gather | solution.py:111
  281.0 2.0 fusion.21
  283.0 2.7 copy.34
  285.7 3.9 %bitcast_reduce_fusion.2 = bf16[384,384]{1,0:T(8,128)(2,1)} fusion(bf16[4,384,2,384]{1,3,2,0:T(8,128)(2,1)} %bitcast.79, bf16[384,384,1]{1,0,2:T(8,128)(2,1)S(1)} %fusion.50, bf16[384,384,1]{1,0,2:T(8,128)(2,1)S(1)} %multiply_convert_fusion.2), kind=kOutput, calls=%fused_computation.36 | convolution fusion | flops 906706944 | bytes 3244032 | tf_op jit(solution)/shard_map/ykc,tkcx->tyx/dot_general | solution.py:77
  289.6 1.7 all-gather.15.cloned.1.call-done
  292.5 18.2 %all-gather.17.cloned.1.call-done = bf16[1536,384]{0,1:T(8,128)(2,1)} async-done(((bf16[384,384]{0,1:T(8,128)(2,1)}), bf16[1536,384]{0,1:T(8,128)(2,1)}) %all-gather.17.cloned.1.call-update) | async-done | bytes 1179664 | tf_op jit(solution)/shard_map/all_gather | solution.py:11
  312.0 18.2 %all-gather.19.cloned.1.call-done = bf16[1536,384]{0,1:T(8,128)(2,1)} async-done(((bf16[384,384]{0,1:T(8,128)(2,1)}), bf16[1536,384]{0,1:T(8,128)(2,1)}) %all-gather.19.cloned.1.call-update) | async-done | bytes 1179664 | tf_op jit(solution)/shard_map/all_gather | solution.py:11
  331.5 2.5 copy.35
  334.0 2.4 copy.36
  336.4 1.4 copy.37
  337.8 11.9 %all-gather.21.cloned.1.call-done = bf16[1536,384]{0,1:T(8,128)(2,1)} async-done(((bf16[384,384]{0,1:T(8,128)(2,1)}), bf16[1536,384]{0,1:T(8,128)(2,1)}) %all-gather.21.cloned.1.call-update) | async-done | bytes 1179664 | tf_op jit(solution)/shard_map/all_gather | solution.py:11
  350.9 2.4 copy.38
  353.3 7.3 %while.21 = (s32[]{:T(128)}, f32[384,384]{1,0:T(8,128)S(1)}, f32[384,384]{1,0:T(8,128)S(1)}, f32[384,384]{1,0:T(8,128)S(1)}, f32[384,384]{1,0:T(8,128)S(1)}, /*i...) while((s32[]{:T(128)}, f32[384,384]{1,0:T(8,128)S(1)}, ...), condition=%wide.region_5.6_spmd, body=%wide.region_4.5_spmd.sunk | while | flops 1179653 | bytes 5898407 | solution.py:23
  354.5 1.2 convert_maximum_fusion.3
  357.0 1.2 convert_maximum_fusion.3
  359.4 1.2 convert_maximum_fusion.3
  (70 shorter events, 18.2 us)
Async XLA Ops:
  7.2 18.9 %copy-start = (bf16[384,384]{1,0:T(8,128)(2,1)S(1)}, bf16[384,384]{1,0:T(8,128)(2,1)}, u32[]{:S(2)}) copy-start(bf16[384,384]{1,0:T(8,128)(2,1)} %param.8) | copy-start | bytes 884740
  7.2 2.4 copy-start.7
  7.2 144.7 %all-gather.11.cloned.1.call-start = ((), (), s32[]{:S(2)}) async-start(), calls=%async_computation | async-start | bytes 10616832 | tf_op jit(solution)/shard_map/all_gather | solution.py:99
  10.9 260.7 %all-gather.13.cloned.1.call-start = ((), (), s32[]{:S(2)}) async-start(), calls=%async_computation.1 | async-start | bytes 23592960 | tf_op jit(solution)/shard_map/all_gather | solution.py:110
  16.3 275.0 %all-gather.15.cloned.1.call-start = ((), (), s32[]{:S(2)}) async-start(), calls=%async_computation.2 | async-start | bytes 1474560 | tf_op jit(solution)/shard_map/all_gather | solution.py:11
  27.8 129.9 %copy-start.4 = (f32[384,384]{1,0:T(8,128)}, f32[384,384]{1,0:T(8,128)S(1)}, u32[]{:S(2)}) copy-start(f32[384,384]{1,0:T(8,128)S(1)} %copy.17) | copy-start | bytes 1769476
  30.2 127.5 %copy-start.8 = (bf16[384,384]{1,0:T(8,128)(2,1)}, bf16[384,384]{1,0:T(8,128)(2,1)S(1)}, u32[]{:S(2)}) copy-start(bf16[384,384]{1,0:T(8,128)(2,1)S(1)} %fusion.53) | copy-start | bytes 884740
  37.5 120.3 %copy-start.10 = (bf16[384,384]{1,0:T(8,128)(2,1)}, bf16[384,384]{1,0:T(8,128)(2,1)S(1)}, u32[]{:S(2)}) copy-start(bf16[384,384]{1,0:T(8,128)(2,1)S(1)} %get-tuple-element.277) | copy-start | bytes 884740
  37.5 120.3 %copy-start.12 = (bf16[384,384]{1,0:T(8,128)(2,1)}, bf16[384,384]{1,0:T(8,128)(2,1)S(1)}, u32[]{:S(2)}) copy-start(bf16[384,384]{1,0:T(8,128)(2,1)S(1)} %get-tuple-element.278) | copy-start | bytes 884740
  180.9 12.9 %copy-start.14 = (s32[4,1]{0,1:T(1,128)S(1)}, s32[4,1]{0,1:T(1,128)}, u32[]{:S(2)}) copy-start(s32[4,1]{0,1:T(1,128)} %param.13) | copy-start | bytes 52
  180.9 12.9 %copy-start.15 = (s32[4,1]{0,1:T(1,128)S(1)}, s32[4,1]{0,1:T(1,128)}, u32[]{:S(2)}) copy-start(s32[4,1]{0,1:T(1,128)} %param.12) | copy-start | bytes 52
  192.5 118.2 %all-gather.17.cloned.1.call-start = ((), (), s32[]{:S(2)}) async-start(), calls=%async_computation.3 | async-start | bytes 1474560 | tf_op jit(solution)/shard_map/all_gather | solution.py:11
  193.1 137.1 %all-gather.19.cloned.1.call-start = ((), (), s32[]{:S(2)}) async-start(), calls=%async_computation.4 | async-start | bytes 1474560 | tf_op jit(solution)/shard_map/all_gather | solution.py:11
  193.7 156.0 %all-gather.21.cloned.1.call-start = ((), (), s32[]{:S(2)}) async-start(), calls=%async_computation.5 | async-start | bytes 1474560 | tf_op jit(solution)/shard_map/all_gather | solution.py:11
  278.7 1.1 copy-start.5
  279.8 1.0 copy-start.9
  279.8 1.1 copy-start.11
  279.8 1.2 copy-start.13
  331.5 4.9 %copy-start.6 = (bf16[1536,384]{0,1:T(8,128)(2,1)S(1)}, bf16[1536,384]{0,1:T(8,128)(2,1)}, u32[]{:S(2)}) copy-start(bf16[1536,384]{0,1:T(8,128)(2,1)} %all-gather.19.cloned.1.call-done) | copy-start | bytes 3538948
  360.6 1.8 copy-start.2
  360.7 1.8 copy-start.3
  360.7 1.8 copy-start.1
Sparse Core Ops, SparseCore 0:
  11.0 140.7 all-gather.10
  153.4 118.1 all-gather.12
  273.8 17.4 all-gather.14
  293.3 17.4 all-gather.16
  312.7 17.4 all-gather.18
  332.2 17.4 all-gather.20
where the time goes:
time: 370 us; the launch traced here: 369 us
  waiting for transfers between devices  243 us (66%)
  other arithmetic  45.9 us (12%)
  local copies, waits for them, and re-layouts  36.2 us (10%)
  matrix products  29 us (8%)
  between operations  14.5 us (4%)
    all_gather x1, waiting for transfers between devices, body(): lax.all_gather(search_filtered, 'mic', axis=1, tiled=True)  114 us
    all_gather x1, waiting for transfers between devices, body(): gathered = lax.all_gather(library_filtered, 'orient', axis=0, tiled=True)  77.9 us
    all_gather x4, waiting for transfers between devices, merged_2(): lax.all_gather(a.astype(kind), axis)  50.1 us
    dot_general x2, matrix products, row_pass(): jnp.einsum('ykc,tkcx->tyx', inv_rows, stacked, preferred_element_type=jnp...  15.5 us
    reshape x2, local copies, waits for them, and re-layouts, row_pass(): stacked = halfway.reshape(halfway.shape[0], box_edge, 2, box_edge)  15.5 us
    dot_general x2, matrix products, column_pass(): jnp.einsum('trl,lm->trm', product, inv_cols, preferred_element_type=jnp.f...  12.3 us
    while x8, local copies, waits for them, and re-layouts, merged_2(): lax.fori_loop(1, lax.axis_size(axis), lambda source, state: join(state, t...  9.6 us
  transfers between devices with their start and end apart: 6, of which 6 were waited for; matrix products, arithmetic and copies ran while one was open for 25% of the time, Pallas kernels for 0%

commit v1 on v0

v1 whole, which is shorter than its diff:
```python
import math

import jax
import jax.numpy as jnp
import numpy as np
from jax import lax
from jax.experimental import pallas as pl
from jax.experimental.pallas import tpu as pltpu
from jax.sharding import PartitionSpec as P


def make_tables(box_edge):
    positions = jnp.arange(box_edge, dtype=jnp.int32)
    products = positions[:, None] * positions[None, :] % box_edge
    angles = products.astype(jnp.float32) * (2.0 * math.pi / box_edge)
    cosine = jnp.cos(angles)
    sines = jnp.sin(angles)
    fwd_cos = cosine.astype(jnp.bfloat16)
    fwd_sin = sines.astype(jnp.bfloat16)
    inv_cos = (cosine / box_edge).astype(jnp.bfloat16)
    inv_sin = (sines / box_edge).astype(jnp.bfloat16)
    fwd_half = jnp.concatenate([fwd_cos, -fwd_sin], axis=1)
    fwd_full = jnp.stack([jnp.stack([fwd_cos, fwd_sin], -1), jnp.stack([-fwd_sin, fwd_cos], -1)], 0)
    inv_cols = jnp.concatenate(
        [jnp.concatenate([inv_cos, inv_sin], 1), jnp.concatenate([-inv_sin, inv_cos], 1)], 0
    )
    inv_rows = jnp.stack([inv_cos, -inv_sin], -1)
    return (fwd_half, fwd_full, inv_cols, inv_rows)


def forward(tile_image, fwd_half, fwd_full):
    box_edge = tile_image.shape[0]
    half_spectrum = jnp.dot(tile_image, fwd_half, preferred_element_type=jnp.float32).astype(
        jnp.bfloat16
    )
    stacked = half_spectrum.reshape(box_edge, 2, box_edge)
    spectrum = jnp.einsum("dykc,kcx->ydx", fwd_full, stacked, preferred_element_type=jnp.float32)
    return spectrum.reshape(box_edge, 2 * box_edge).astype(jnp.bfloat16)


def fold_matrices(edge):
    half = edge // 2
    own = np.zeros((2 * edge, edge), np.float32)
    mirror = np.zeros((2 * edge, edge), np.float32)
    for l in range(1, half):
        own[l, l] = 1.0
        own[edge + l, half + l] = 1.0
        mirror[edge - l, l] = 1.0
        mirror[2 * edge - l, half + l] = -1.0
    own[0, 0], own[edge + half, 0] = 0.5, -0.5
    own[edge, half], own[half, half] = 0.5, 0.5
    mirror[0, 0], mirror[edge + half, 0] = 0.5, 0.5
    mirror[edge, half], mirror[half, half] = -0.5, 0.5
    return jnp.asarray(own, jnp.bfloat16), jnp.asarray(mirror, jnp.bfloat16)


def gather_half(filtered):
    count, rows, width = filtered.shape
    edge = width // 2
    mics = lax.axis_size("mic")
    own_map, mirror_map = fold_matrices(edge)
    mirrored = jnp.einsum(
        "tkc,cl->tkl", filtered, mirror_map, preferred_element_type=jnp.float32
    ).astype(jnp.bfloat16)
    flip = np.zeros((rows, rows), np.float32)
    for i in range(1, rows):
        flip[i, rows - i] = 1.0
    turned = jnp.einsum(
        "ik,tkl->til", jnp.asarray(flip, jnp.bfloat16), mirrored, preferred_element_type=jnp.float32
    ).astype(jnp.bfloat16)
    first = lax.ppermute(mirrored[:, 0, :], "mic", [(m, (mics - m) % mics) for m in range(mics)])
    rest = lax.ppermute(turned, "mic", [(m, mics - 1 - m) for m in range(mics)])
    own = jnp.einsum("tkc,cl->tkl", filtered, own_map, preferred_element_type=jnp.float32)
    row = lax.broadcasted_iota(jnp.int32, (1, rows, 1), 1)
    other = jnp.where(row == 0, first[:, None, :].astype(jnp.float32), rest.astype(jnp.float32))
    folded = (own + other).astype(jnp.bfloat16)
    if rows % 16 == 0:
        return lax.all_gather(folded, "mic", axis=0)
    return lax.all_gather(folded, "mic", axis=1, tiled=True)[None]


def search_kernel(
    e_ref, gr_ref, gi_ref, gb_ref, cs_ref, col_ref, flip_ref, peak_ref, total_ref, square_ref
):
    step = pl.program_id(0)
    edge = gr_ref.shape[0]
    half = edge // 2
    e_bf = e_ref[...].reshape(edge, edge)
    e = e_bf.astype(jnp.float32)
    es = jnp.concatenate([e[:, half:], e[:, :half]], axis=1)
    gr = gr_ref[...]
    gi = gi_ref[...]
    lane = lax.broadcasted_iota(jnp.int32, (edge, edge), 1)
    low = lane < half
    narrow = lax.broadcasted_iota(jnp.int32, (edge, 128), 1)
    dr = jnp.dot(
        flip_ref[...],
        jnp.where(narrow == 0, e[:, :128], pltpu.roll(es[:, :128], 1, 1)).astype(jnp.bfloat16),
        preferred_element_type=jnp.float32,
    )
    gbr, gbi = gb_ref[:, 0:1], gb_ref[:, 1:2]
    mr, mi = dr[:, 0:1], dr[:, 1:2]
    fix_r = gbr * mr - gbi * mi
    fix_i = gbr * mi + gbi * mr
    ge, ges = gr * e, gr * es
    he, hes = gi * e, gi * es
    top = jnp.where(low, ge, -ge) + hes
    bottom = ges + jnp.where(low, -he, he)
    at_r, at_i = lane == 0, lane == half
    top = top + jnp.where(at_r, fix_r, jnp.where(at_i, fix_i, 0.0))
    bottom = bottom + jnp.where(at_r, -fix_i, jnp.where(at_i, fix_r, 0.0))
    stacked = jnp.concatenate([top.astype(jnp.bfloat16), bottom.astype(jnp.bfloat16)], axis=0)
    v = jnp.dot(cs_ref[...], stacked, preferred_element_type=jnp.float32).astype(jnp.bfloat16)
    corr = jnp.dot(v, col_ref[...], preferred_element_type=jnp.float32)

    @pl.when(step == 0)
    def _():
        peak_ref[...] = corr
        total_ref[...] = corr
        square_ref[...] = corr * corr

    @pl.when(step > 0)
    def _():
        peak_ref[...] = jnp.maximum(peak_ref[...], corr)
        total_ref[...] += corr
        square_ref[...] += corr * corr


def search_maps(gathered, gr, gi, gb, cs, col):
    mics, count, rows, edge = gathered.shape
    flip = np.zeros((edge, edge), np.float32)
    for k in range(edge):
        flip[k, (edge - k) % edge] = 1.0
    whole = lambda a: pl.BlockSpec(a.shape, lambda t: (0, 0))
    flip = jnp.asarray(flip, jnp.bfloat16)
    out = jax.ShapeDtypeStruct((edge, edge), jnp.float32)
    return pl.pallas_call(
        search_kernel,
        grid=(count,),
        in_specs=[pl.BlockSpec((mics, 1, rows, edge), lambda t: (0, t, 0, 0))]
        + [whole(a) for a in (gr, gi, gb, cs, col, flip)],
        out_specs=[pl.BlockSpec((edge, edge), lambda t: (0, 0))] * 3,
        out_shape=[out] * 3,
        compiler_params=pltpu.CompilerParams(vmem_limit_bytes=40 * 1024 * 1024),
        cost_estimate=pl.CostEstimate(flops=count * 350000000, bytes_accessed=count * 600000, transcendentals=0),
    )(gathered, gr, gi, gb, cs, col, flip)


def refine_kernel(lib_ref, ctf_ref, g_ref, cs_ref, col_ref, wanted_ref, out_ref):
    step = pl.program_id(0)
    edge = ctf_ref.shape[0]

    @pl.when(step == 0)
    def _():
        out_ref[...] = jnp.full((edge, edge), -3.0e38, jnp.float32)

    @pl.when(wanted_ref[step] > 0)
    def _():
        gain = ctf_ref[...]
        fr = (lib_ref[0, :, :edge].astype(jnp.float32) * gain).astype(jnp.bfloat16).astype(jnp.float32)
        fi = (lib_ref[0, :, edge:].astype(jnp.float32) * gain).astype(jnp.bfloat16).astype(jnp.float32)
        gr = g_ref[:, :edge].astype(jnp.float32)
        gi = g_ref[:, edge:].astype(jnp.float32)
        zr = (gr * fr + gi * fi).astype(jnp.bfloat16)
        zi = (gi * fr - gr * fi).astype(jnp.bfloat16)
        ci, si = cs_ref[:, :edge], cs_ref[:, edge:]
        dot = lambda a, b: jnp.dot(a, b, preferred_element_type=jnp.float32)
        ur = (dot(ci, zr) - dot(si, zi)).astype(jnp.bfloat16)
        ui = (dot(si, zr) + dot(ci, zi)).astype(jnp.bfloat16)
        corr = dot(ur, col_ref[:edge]) - dot(ui, col_ref[edge:])
        out_ref[...] = jnp.maximum(out_ref[...], corr)


def refine_map(library, ctf, spectrum, cs, col, wanted):
    count, edge, width = library.shape
    whole = lambda a: pl.BlockSpec(a.shape, lambda t: (0, 0))
    return pl.pallas_call(
        refine_kernel,
        grid=(count,),
        in_specs=[pl.BlockSpec((1, edge, width), lambda t: (t, 0, 0))]
        + [whole(a) for a in (ctf, spectrum, cs, col)]
        + [pl.BlockSpec(memory_space=pltpu.SMEM)],
        out_specs=pl.BlockSpec((edge, edge), lambda t: (0, 0)),
        out_shape=jax.ShapeDtypeStruct((edge, edge), jnp.float32),
        compiler_params=pltpu.CompilerParams(vmem_limit_bytes=40 * 1024 * 1024),
        cost_estimate=pl.CostEstimate(flops=count * 700000000, bytes_accessed=count * 1200000, transcendentals=0),
    )(library, ctf, spectrum, cs, col, wanted)


def join(left, right):
    low = jnp.maximum(left[0], right[0].astype(jnp.float32))
    total = left[1] + right[1].astype(jnp.float32)
    square = left[2] + right[2].astype(jnp.float32)
    return (low, total, square, jnp.maximum(left[3], right[3].astype(jnp.float32)))


def merge(maps):
    size = lax.axis_size("orient")
    edge = maps[0].shape[0]
    half = edge // 2
    core = lax.axis_index("orient") % 2
    near = [(i, i ^ 1) for i in range(size)]
    narrow = lambda values: [a.astype(jnp.bfloat16) for a in values]
    mine = [lax.dynamic_slice_in_dim(a, core * half, half, 0) for a in maps]
    theirs = narrow(lax.dynamic_slice_in_dim(a, (1 - core) * half, half, 0) for a in maps)
    state = join(mine, lax.ppermute(jnp.stack(theirs), "orient", near))
    distance = 2
    while distance < size:
        far = [(i, i ^ distance) for i in range(size)]
        state = join(state, lax.ppermute(jnp.stack(narrow(state)), "orient", far))
        distance *= 2
    final = jnp.stack(narrow(state))
    other = lax.ppermute(final, "orient", near)
    first = jnp.where(core == 0, final, other)
    second = jnp.where(core == 0, other, final)
    return [jnp.concatenate([first[i], second[i]], 0).astype(jnp.float32) for i in range(4)]


def body(micrograph, search_spectra, refine_spectra, ctf, ref_owner, ref_slot):
    edge = micrograph.shape[1]
    half = edge // 2
    fwd_half, fwd_full, inv_cols, _ = make_tables(edge)
    ctf_gain = jnp.concatenate([ctf, ctf], 1)
    rows_owned = search_spectra.shape[1]
    first_row = lax.axis_index("mic") * rows_owned
    own_gain = lax.dynamic_slice_in_dim(ctf_gain, first_row, rows_owned, 0)
    filtered = (search_spectra.astype(jnp.float32) * own_gain).astype(jnp.bfloat16)
    gathered = gather_half(filtered)
    spectrum = forward(micrograph, fwd_half, fwd_full)

    library = refine_spectra[0]
    block_size = library.shape[0]
    ids = lax.all_gather(ref_owner[:, 0] * block_size + ref_slot[:, 0], "orient", axis=0, tiled=True)
    slots = lax.axis_index("orient") * block_size + jnp.arange(block_size, dtype=jnp.int32)
    wanted = jnp.any(slots[:, None] == ids[None, :], axis=1).astype(jnp.int32)
    cs = inv_cols[:edge]
    inv_cos, inv_sin = inv_cols[:edge, :edge], inv_cols[:edge, edge:]
    refine_cols = jnp.concatenate([inv_cos, inv_sin], 0)
    refined = refine_map(library, ctf, spectrum, cs, refine_cols, wanted)

    spec = spectrum.astype(jnp.float32)
    g_r, g_i = spec[:, :edge], spec[:, edge:]
    dc = jnp.stack([g_r[:, 0], g_i[:, 0]], 1)
    ny = jnp.stack([g_r[:, half], g_i[:, half]], 1)
    ga = (dc - ny) * 0.5
    gb = (dc + ny) * 0.5
    lane = lax.broadcasted_iota(jnp.int32, (edge, half), 1)
    h_r = jnp.where(lane == 0, ga[:, 0:1], g_r[:, :half])
    h_i = jnp.where(lane == 0, ga[:, 1:2], g_i[:, :half])
    gr = jnp.concatenate([h_r, h_r], 1)
    gi = jnp.concatenate([h_i, h_i], 1)
    row = lax.broadcasted_iota(jnp.int32, (half, edge), 0)
    sin_rows = jnp.where(row == 0, inv_cos[half : half + 1], -inv_sin[:half])
    col = jnp.concatenate([inv_cos[:half], sin_rows], 0)
    peak, total, square = search_maps(gathered, gr, gi, gb, cs, col)
    peak, total, square, refined = merge([peak, total, square, refined])
    count = float(lax.axis_size("orient") * search_spectra.shape[0])
    return (peak, total / count, peak * lax.rsqrt(square / count + 1e-05), refined)


def solution(mesh):
    in_specs = (
        P("mic", None),
        P("orient", "mic", None),
        P("mic", "orient", None, None),
        P(),
        P(("mic", "orient"), None),
        P(("mic", "orient"), None),
    )
    out_specs = (P("mic", None), P("mic", None), P("mic", None), P("mic", None))
    return jax.shard_map(body, mesh=mesh, in_specs=in_specs, out_specs=out_specs, check_vma=False)
```

time: 370 us -> 186 us (0.50)
  waiting for transfers between devices: 243 us -> 89.2 us
  Pallas kernels: 0 us -> 31.4 us
  local copies, waits for them, and re-layouts: 36.2 us -> 10.8 us
  other arithmetic: 45.9 us -> 20.7 us
  matrix products: 29 us -> 5.37 us
  starting transfers between devices: 0.24 us -> 8.36 us
  blocking collectives: 0 us -> 4.94 us
    all_gather x6 -> x1, waiting for transfers between devices: 242 us -> 58.3 us  [gather_half(): return lax.all_gather(folded, 'mic', axis=0)]
    pallas_call x0 -> x2, Pallas kernels: none -> 31.4 us  [the longest x1 26.4 us: search_maps(): pl.pallas_call(search_kernel, grid=(count,), in_specs=[pl.BlockSpec((mics...]
    ppermute x0 -> x5, waiting for transfers between devices: none -> 30.9 us  [the longest x1 13.9 us: merge(): state = join(state, lax.ppermute(jnp.stack(narrow(state)), 'orient', far))]
    dot_general x4 -> x3, matrix products: 27.8 us -> 4.16 us  [the longest x1 2.26 us: gather_half(): jnp.einsum('tkc,cl->tkl', filtered, mirror_map, preferred_element_type=jn...]
    reshape x2 -> x0, local copies, waits for them, and re-layouts: 15.5 us -> none  [row_pass(): stacked = halfway.reshape(halfway.shape[0], box_edge, 2, box_edge)]
    while x8 -> x0, local copies, waits for them, and re-layouts: 9.6 us -> none  [merged_2(): lax.fori_loop(1, lax.axis_size(axis), lambda source, state: join(state, t...]
    convert_element_type x8 -> x5, other arithmetic: 13 us -> 4.53 us  [the longest x1 2.55 us: make_tables(): fwd_sin = sines.astype(jnp.bfloat16)]
    ppermute x0 -> x5, starting transfers between devices: none -> 8.32 us  [the longest x1 6.05 us: gather_half(): rest = lax.ppermute(turned, 'mic', [(m, mics - 1 - m) for m in range(mics)])]
  transfers between devices with their start and end apart: 6 -> 6, of which waited for: 6 -> 5; matrix products, arithmetic and copies ran while one was open for 25% -> 10% of each run, Pallas kernels for 0% -> 3%
where the time goes in v1:
time: 186 us
  waiting for transfers between devices  89.2 us (48%)
  Pallas kernels  31.4 us (17%)
  other arithmetic  20.7 us (11%)
  between operations  15.2 us (8%)
  local copies, waits for them, and re-layouts  10.8 us (6%)
  starting transfers between devices  8.36 us (4%)
  matrix products  5.37 us (3%)
  blocking collectives  4.94 us (3%)
    all_gather x1, waiting for transfers between devices, gather_half(): return lax.all_gather(folded, 'mic', axis=0)  58.3 us
    pallas_call x1, Pallas kernels, search_maps(): pl.pallas_call(search_kernel, grid=(count,), in_specs=[pl.BlockSpec((mics...  26.4 us
    ppermute x1, waiting for transfers between devices, merge(): state = join(state, lax.ppermute(jnp.stack(narrow(state)), 'orient', far))  13.9 us
    ppermute x1, waiting for transfers between devices, gather_half(): rest = lax.ppermute(turned, 'mic', [(m, mics - 1 - m) for m in range(mics)])  12.8 us
    unnamed x39, local copies, waits for them, and re-layouts  9.12 us
    ppermute x1, starting transfers between devices, gather_half(): rest = lax.ppermute(turned, 'mic', [(m, mics - 1 - m) for m in range(mics)])  6.05 us
    pallas_call x1, Pallas kernels, refine_map(): pl.pallas_call(refine_kernel, grid=(count,), in_specs=[pl.BlockSpec((1, e...  5.07 us
    unnamed x1, blocking collectives  4.94 us
  transfers between devices with their start and end apart: 6, of which 5 were waited for; matrix products, arithmetic and copies ran while one was open for 10% of the time, Pallas kernels for 3%

profile of v1, /device:TPU:0, one launch (start us, length us, event | category | flops | bytes accessed | tf_op | source)
XLA Modules:
  0.0 185.9 jit_solution(4851848931490174169)
XLA Ops:
  7.2 1.0 fusion.44
  8.2 2.3 %convolution_convert_fusion.2 = bf16[16,48,384]{2,1,0:T(8,128)(2,1)S(1)} fusion(bf16[768,384,1]{1,0,2:T(8,128)(2,1)} %constant.83, bf16[16,48,768]{2,1,0:T(8,128)(2,1)} %param.11, f32[48,768]{1,0:T(8,128)S(1)} %fusion.44), kind=kOutput, calls=%fused_computation.5 | convolution fusion | flops 455049216 | bytes 2506752 | tf_op jit(solution)/shard_map/tkc,cl->tkl/dot_general | solution.py:62
  10.8 6.0 %collective-permute-start.1 = (bf16[16,48,384]{2,1,0:T(8,128)(2,1)S(1)}, bf16[16,48,384]{2,1,0:T(8,128)(2,1)S(1)}, u32[]{:S(2)}, u32[]{:S(2)}) collective-permute-start(bf16[16,48,384]{2,1,0:T(8,128)(2,1)S(1)} %fusion.1), channel_id=1, source_target_pairs={{0,28},{4,24},{8,20},{12,16},{16,12},{20,8},{24,4},{28,0},{1,29},{... | collective-permute-start | bytes 1769480 | tf_op jit(solution)/shard_map/ppermute | solution.py:72
  16.9 0.7 collective-permute-start
  17.6 12.8 %collective-permute-done.1 = bf16[16,48,384]{2,1,0:T(8,128)(2,1)S(1)} collective-permute-done((bf16[16,48,384]{2,1,0:T(8,128)(2,1)S(1)}, bf16[16,48,384]{2,1,0:T(8,128)(2,1)S(1)}, u32[]{:S(2)}, u32[]{:S(2)}) %collective-permute-start.1) | collective-permute-done | bytes 589856 | tf_op jit(solution)/shard_map/ppermute | solution.py:72
  30.4 1.6 add_convert_fusion
  33.5 4.9 %all-reduce = s32[16]{0:T(128)S(1)} all-reduce(s32[16]{0:T(128)S(1)} %bitcast_dynamic-update-slice_fusion), channel_id=3, replica_groups=mesh['mic'=8,'orient'=4] {'orient'}, use_global_device_ids=true, to_apply=%add | all-reduce | flops 16 | bytes 128
  38.6 2.3 %fusion.46 = bf16[384,384,1]{1,0,2:T(8,128)(2,1)S(1)} fusion(), kind=kLoop, calls=%fused_computation.115 | loop fusion | flops 1916928 | bytes 294912 | tf_op jit(solution)/shard_map/neg | solution.py:22
  40.9 2.3 %fusion.23 = bf16[384,384]{1,0:T(8,128)(2,1)S(1)} fusion(), kind=kLoop, calls=%fused_computation.54 | loop fusion | flops 1916928 | bytes 294912 | tf_op jit(solution)/shard_map/neg | solution.py:22
  43.3 2.3 %fusion.19 = bf16[384,384]{1,0:T(8,128)(2,1)S(1)} fusion(), kind=kLoop, calls=%fused_computation.46 | loop fusion | flops 1474560 | bytes 294912 | tf_op jit(solution)/shard_map/convert_element_type | solution.py:18
  45.6 2.6 %sine_convert_fusion = (bf16[384,384,1]{1,0,2:T(8,128)(2,1)S(1)}, bf16[384,384,1]{1,0,2:T(8,128)(2,1)S(1)}) fusion(), kind=kLoop, calls=%fused_computation.36 | loop fusion | flops 1622016 | bytes 589824 | tf_op jit(solution)/shard_map/convert_element_type | solution.py:19
  49.8 2.6 %multiply_convert_fusion.3 = (bf16[384,384]{1,0:T(8,128)(2,1)S(1)}, bf16[384,384]{1,0:T(8,128)(2,1)S(1)}) fusion(), kind=kLoop, calls=%fused_computation.34 | loop fusion | flops 1916928 | bytes 589824 | tf_op jit(solution)/shard_map/convert_element_type | solution.py:21
  52.4 1.1 convert_element_type.247
  53.7 0.9 copy-done.1
  54.6 2.3 %copy-done.7 = bf16[1,8,384,768]{3,2,1,0:T(8,128)(2,1)S(1)} copy-done((bf16[1,8,384,768]{3,2,1,0:T(8,128)(2,1)S(1)}, bf16[1,8,384,768]{3,2,1,0:T(8,128)(2,1)}, u32[]{:S(2)}) %copy-start.7) | copy-done | bytes 4718616
  56.9 5.1 %shard_map.130 = f32[384,384]{1,0:T(8,128)S(1)} custom-call(bf16[8,384,768]{2,1,0:T(8,128)(2,1)S(1)} %bitcast.124, f32[384,384]{1,0:T(8,128)S(1)} %copy-done.1, bf16[384,768]{1,0:T(8,128)(2,1)S(1)} %copy.27.g_ref, bf16[384,768]{1,0:T(8,128)(2,1)S(1)} %pad_maximum_fusion.2.cs_ref, bf16[768,384]{1,0:T(8,128)(2,1)S(1)} %pad_maximum_fusion.3.col_ref, ...), custom_call_target="tpu_custom_call" | custom-call | flops 5600000000 | bytes 9600000 | tf_op jit(solution)/shard_map/pallas_call | solution.py:177
  62.0 0.8 fusion.39
  63.1 0.9 add_multiply_fusion
  64.9 58.3 %all-gather.4.cloned.1.call-done = bf16[128,48,384]{2,1,0:T(8,128)(2,1)} async-done(((bf16[16,48,384]{2,1,0:T(8,128)(2,1)}), bf16[128,48,384]{2,1,0:T(8,128)(2,1)}) %all-gather.4.cloned.1.call-update) | async-done | bytes 4718608 | tf_op jit(solution)/shard_map/all_gather | solution.py:78
  123.2 0.9 copy-done.6
  124.1 2.3 %copy-done.8 = bf16[128,48,384]{2,1,0:T(8,128)(2,1)S(1)} copy-done((bf16[128,48,384]{2,1,0:T(8,128)(2,1)S(1)}, bf16[128,48,384]{2,1,0:T(8,128)(2,1)}, u32[]{:S(2)}) %copy-start.8) | copy-done | bytes 4718616
  126.4 1.0 copy-done.9
  127.4 26.4 %shard_map.129 = (f32[384,384]{1,0:T(8,128)S(1)}, f32[384,384]{1,0:T(8,128)S(1)}, f32[384,384]{1,0:T(8,128)S(1)}) custom-call(bf16[8,16,48,384]{3,2,1,0:T(8,128)(2,1)S(1)} %bitcast.125, f32[384,384]{1,0:T(8,128)S(1)} %pad_maximum_fusion.gr_ref, f32[384,384]{1,0:T(8,128)S(1)} %pad_maximum_fusion.1.gi_ref, f32[384,2]{1,0:T(8,128)S(1)} %copy-done.6, ...), custom_call_target="tpu_custom_call" | custom-call | flops 5600000000 | bytes 9600000 | tf_op jit(solution)/shard_map/pallas_call | solution.py:137
  153.9 0.7 copy-done.4
  154.6 0.9 pad_maximum_fusion.4
  155.6 2.2 %collective-permute-done.2 = bf16[4,192,384]{2,1,0:T(8,128)(2,1)S(1)} collective-permute-done((bf16[4,192,384]{2,1,0:T(8,128)(2,1)}, bf16[4,192,384]{2,1,0:T(8,128)(2,1)S(1)}, u32[]{:S(2)}, u32[]{:S(2)}) %collective-permute-start.2) | collective-permute-done | bytes 589856 | tf_op jit(solution)/shard_map/ppermute | solution.py:206
  158.1 1.5 collective-permute-start.3
  159.6 13.9 %collective-permute-done.3 = bf16[4,192,384]{2,1,0:T(8,128)(2,1)S(1)} collective-permute-done((bf16[4,192,384]{2,1,0:T(8,128)(2,1)S(1)}, bf16[4,192,384]{2,1,0:T(8,128)(2,1)S(1)}, u32[]{:S(2)}, u32[]{:S(2)}) %collective-permute-start.3) | collective-permute-done | bytes 589856 | tf_op jit(solution)/shard_map/ppermute | solution.py:210
  173.9 2.0 %collective-permute-done.4 = bf16[4,192,384]{2,1,0:T(8,128)(2,1)S(1)} collective-permute-done((bf16[4,192,384]{2,1,0:T(8,128)(2,1)S(1)}, bf16[4,192,384]{2,1,0:T(8,128)(2,1)S(1)}, u32[]{:S(2)}, u32[]{:S(2)}) %collective-permute-start.4) | collective-permute-done | bytes 589856 | tf_op jit(solution)/shard_map/ppermute | solution.py:213
  176.2 0.9 maximum_convert_fusion.1
  177.0 0.9 convert_multiply_fusion
  177.9 1.1 rsqrt_multiply_fusion
  (74 shorter events, 5.3 us)
Async XLA Ops:
  7.2 41.1 %copy-start = (bf16[384,384]{1,0:T(8,128)(2,1)S(1)}, bf16[384,384]{1,0:T(8,128)(2,1)}, u32[]{:S(2)}) copy-start(bf16[384,384]{1,0:T(8,128)(2,1)} %param.10) | copy-start | bytes 884740
  7.2 116.0 %all-gather.4.cloned.1.call-start = ((), (), s32[]{:S(2)}) async-start(), calls=%async_computation | async-start | bytes 5308416 | tf_op jit(solution)/shard_map/all_gather | solution.py:78
  8.2 2.3 %copy-start.12 = (bf16[48,48,1]{1,0,2:T(8,128)(2,1)S(1)}, bf16[48,48,1]{1,0,2:T(8,128)(2,1)}, u32[]{:S(2)}) copy-start(bf16[48,48,1]{1,0,2:T(8,128)(2,1)} %constant.84) | copy-start | bytes 13828
  8.2 22.2 %copy-start.16 = (bf16[768,384,1]{1,0,2:T(8,128)(2,1)S(1)}, bf16[768,384,1]{1,0,2:T(8,128)(2,1)}, u32[]{:S(2)}) copy-start(bf16[768,384,1]{1,0,2:T(8,128)(2,1)} %constant.82) | copy-start | bytes 1769476
  10.5 19.9 %copy-start.15 = (bf16[16,48,768]{2,1,0:T(8,128)(2,1)S(1)}, bf16[16,48,768]{2,1,0:T(8,128)(2,1)}, u32[]{:S(2)}) copy-start(bf16[16,48,768]{2,1,0:T(8,128)(2,1)} %param.11) | copy-start | bytes 3538948
  10.8 19.6 %collective-permute-start.1 = (bf16[16,48,384]{2,1,0:T(8,128)(2,1)S(1)}, bf16[16,48,384]{2,1,0:T(8,128)(2,1)S(1)}, u32[]{:S(2)}, u32[]{:S(2)}) collective-permute-start(bf16[16,48,384]{2,1,0:T(8,128)(2,1)S(1)} %fusion.1), channel_id=1, source_target_pairs={{0,28},{4,24},{8,20},{12,16},{16,12},{20,8},{24,4},{28,0},{1,29},{... | collective-permute-start | bytes 1769480 | tf_op jit(solution)/shard_map/ppermute | solution.py:72
  16.9 0.7 collective-permute-start
  17.6 14.5 %copy-start.17 = (u32[32]{0:T(128)S(1)}, u32[32]{0:T(128)}, u32[]{:S(2)}) copy-start(u32[32]{0:T(128)} %constant.78) | copy-start | bytes 388
  17.6 15.7 %copy-start.13 = (s32[4,1]{0,1:T(1,128)S(1)}, s32[4,1]{0,1:T(1,128)}, u32[]{:S(2)}) copy-start(s32[4,1]{0,1:T(1,128)} %param.15) | copy-start | bytes 52
  17.6 15.7 %copy-start.14 = (s32[4,1]{0,1:T(1,128)S(1)}, s32[4,1]{0,1:T(1,128)}, u32[]{:S(2)}) copy-start(s32[4,1]{0,1:T(1,128)} %param.14) | copy-start | bytes 52
  53.5 1.1 copy-start.1
  54.6 2.3 %copy-start.7 = (bf16[1,8,384,768]{3,2,1,0:T(8,128)(2,1)S(1)}, bf16[1,8,384,768]{3,2,1,0:T(8,128)(2,1)}, u32[]{:S(2)}) copy-start(bf16[1,8,384,768]{3,2,1,0:T(8,128)(2,1)} %param.12) | copy-start | bytes 14155780
  62.0 1.0 copy-start.2
  63.1 1.3 copy-start.10
  123.2 0.9 copy-start.6
  124.1 2.3 %copy-start.8 = (bf16[128,48,384]{2,1,0:T(8,128)(2,1)S(1)}, bf16[128,48,384]{2,1,0:T(8,128)(2,1)}, u32[]{:S(2)}) copy-start(bf16[128,48,384]{2,1,0:T(8,128)(2,1)} %all-gather.4.cloned.1.call-done) | copy-start | bytes 14155780
  126.4 1.0 copy-start.9
  127.4 27.2 %copy-start.11 = (bf16[1,192,384]{2,1,0:T(8,128)(2,1)S(1)}, bf16[1,192,384]{2,1,0:T(8,128)(2,1)}, u32[]{:S(2)}) copy-start(bf16[1,192,384]{2,1,0:T(8,128)(2,1)} %fusion.39) | copy-start | bytes 442372
  153.8 0.8 copy-start.4
  154.6 3.2 %copy-start.3 = (f32[384,384]{1,0:T(8,128)S(1)}, f32[384,384]{1,0:T(8,128)}, u32[]{:S(2)}) copy-start(f32[384,384]{1,0:T(8,128)} %copy-done.2) | copy-start | bytes 1769476
  154.6 3.2 %copy-start.5 = (f32[384,384]{1,0:T(8,128)S(1)}, f32[384,384]{1,0:T(8,128)}, u32[]{:S(2)}) copy-start(f32[384,384]{1,0:T(8,128)} %copy-done.4) | copy-start | bytes 1769476
  155.6 2.2 %collective-permute-start.2 = (bf16[4,192,384]{2,1,0:T(8,128)(2,1)}, bf16[4,192,384]{2,1,0:T(8,128)(2,1)S(1)}, u32[]{:S(2)}, u32[]{:S(2)}) collective-permute-start(bf16[4,192,384]{2,1,0:T(8,128)(2,1)} %pad_maximum_fusion.4), channel_id=1, source_target_pairs={{0,1},{1,0},{2,3},{3,2},{4,5},{5,4},{6,7},{7,6},{8,9},{9,8},{10,11... | collective-permute-start | bytes 1769480 | tf_op jit(solution)/shard_map/ppermute | solution.py:206
  158.1 15.4 %collective-permute-start.3 = (bf16[4,192,384]{2,1,0:T(8,128)(2,1)S(1)}, bf16[4,192,384]{2,1,0:T(8,128)(2,1)S(1)}, u32[]{:S(2)}, u32[]{:S(2)}) collective-permute-start(bf16[4,192,384]{2,1,0:T(8,128)(2,1)S(1)} %pad_maximum_fusion.5), channel_id=1, source_target_pairs={{0,2},{1,3},{2,0},{3,1},{4,6},{5,7},{6,4},{7,5},{8,10},{9,11},{10,... | collective-permute-start | bytes 1769480 | tf_op jit(solution)/shard_map/ppermute | solution.py:210
  173.8 2.1 %collective-permute-start.4 = (bf16[4,192,384]{2,1,0:T(8,128)(2,1)S(1)}, bf16[4,192,384]{2,1,0:T(8,128)(2,1)S(1)}, u32[]{:S(2)}, u32[]{:S(2)}) collective-permute-start(bf16[4,192,384]{2,1,0:T(8,128)(2,1)S(1)} %pad_maximum_fusion.6), channel_id=1, source_target_pairs={{0,1},{1,0},{2,3},{3,2},{4,5},{5,4},{6,7},{7,6},{8,9},{9,8},{10,11... | collective-permute-start | bytes 1769480 | tf_op jit(solution)/shard_map/ppermute | solution.py:213
Sparse Core Ops, SparseCore 0:
  32.2 90.9 all-gather.3

commit v2 on v1

v2 whole, which is shorter than its diff:
```python
import functools
import math

import jax
import jax.numpy as jnp
import numpy as np
from jax import lax
from jax.experimental import pallas as pl
from jax.experimental.pallas import tpu as pltpu
from jax.sharding import PartitionSpec as P

GROUPS = 4


def make_tables(box_edge):
    positions = np.arange(box_edge, dtype=np.int32)
    products = positions[:, None] * positions[None, :] % box_edge
    angles = products.astype(np.float32) * np.float32(2.0 * math.pi / box_edge)
    cosine = np.cos(angles)
    sines = np.sin(angles)
    narrow = lambda a: a.astype(np.float32).astype(jnp.bfloat16)
    fwd_cos, fwd_sin = narrow(cosine), narrow(sines)
    inv_cos = narrow(cosine / np.float32(box_edge))
    inv_sin = narrow(sines / np.float32(box_edge))
    return (fwd_cos, fwd_sin, inv_cos, inv_sin)


def forward(tile_image, fwd_cos, fwd_sin):
    box_edge = tile_image.shape[0]
    full_map = jnp.asarray(np.concatenate([fwd_cos, fwd_sin], 1))
    halved = jnp.dot(tile_image, full_map, preferred_element_type=jnp.float32).astype(jnp.bfloat16)
    ar, ai = halved[:, :box_edge], -halved[:, box_edge:]
    stacked = jnp.concatenate(
        [jnp.concatenate([ar, ai], 1), jnp.concatenate([ai, -ar], 1)], 0
    )
    return jnp.dot(full_map, stacked, preferred_element_type=jnp.float32).astype(jnp.bfloat16)


def fold_matrices(edge):
    half = edge // 2
    mirror = np.zeros((2 * edge, edge), np.float32)
    for l in range(1, half):
        mirror[edge - l, l] = 1.0
        mirror[2 * edge - l, half + l] = -1.0
    mirror[0, 0], mirror[edge + half, 0] = 0.5, 0.5
    mirror[edge, half], mirror[half, half] = -0.5, 0.5
    row = lax.broadcasted_iota(jnp.int32, (2 * edge, edge), 0)
    col = lax.broadcasted_iota(jnp.int32, (2 * edge, edge), 1)
    own = jnp.where(row == jnp.where(col < half, col, col + half), 1.0, 0.0)
    first = jnp.where(row == 0, 0.5, jnp.where(row == edge + half, -0.5, 0.0))
    middle = jnp.where((row == edge) | (row == half), 0.5, 0.0)
    own = jnp.where(col == 0, first, jnp.where(col == half, middle, own))
    return own.astype(jnp.bfloat16), jnp.asarray(mirror, jnp.bfloat16)


def fold_half(filtered):
    count, rows, width = filtered.shape
    edge = width // 2
    mics = lax.axis_size("mic")
    own_map, mirror_map = fold_matrices(edge)
    mirrored = jnp.einsum(
        "tkc,cl->tkl", filtered, mirror_map, preferred_element_type=jnp.float32
    ).astype(jnp.bfloat16)
    flip = np.zeros((rows, rows), np.float32)
    for i in range(1, rows):
        flip[i, rows - i] = 1.0
    turned = jnp.einsum(
        "ik,tkl->til", jnp.asarray(flip, jnp.bfloat16), mirrored, preferred_element_type=jnp.float32
    ).astype(jnp.bfloat16)
    first = lax.ppermute(mirrored[:, 0, :], "mic", [(m, (mics - m) % mics) for m in range(mics)])
    rest = lax.ppermute(turned, "mic", [(m, mics - 1 - m) for m in range(mics)])
    own = jnp.einsum("tkc,cl->tkl", filtered, own_map, preferred_element_type=jnp.float32)
    row = lax.broadcasted_iota(jnp.int32, (1, rows, 1), 1)
    other = jnp.where(row == 0, first[:, None, :].astype(jnp.float32), rest.astype(jnp.float32))
    return (own + other).astype(jnp.bfloat16)


def correlate(e, gr_ref, gi_ref, gb_ref, cs_ref, col_ref, flip_ref):
    edge = gr_ref.shape[0]
    half = edge // 2
    es = jnp.concatenate([e[:, half:], e[:, :half]], axis=1)
    gr = gr_ref[...]
    gi = gi_ref[...]
    lane = lax.broadcasted_iota(jnp.int32, (edge, edge), 1)
    low = lane < half
    narrow = lax.broadcasted_iota(jnp.int32, (edge, 128), 1)
    dr = jnp.dot(
        flip_ref[...],
        jnp.where(narrow == 0, e[:, :128], pltpu.roll(es[:, :128], 1, 1)).astype(jnp.bfloat16),
        preferred_element_type=jnp.float32,
    )
    gbr, gbi = gb_ref[:, 0:1], gb_ref[:, 1:2]
    mr, mi = dr[:, 0:1], dr[:, 1:2]
    fix_r = gbr * mr - gbi * mi
    fix_i = gbr * mi + gbi * mr
    ge, ges = gr * e, gr * es
    he, hes = gi * e, gi * es
    top = jnp.where(low, ge, -ge) + hes
    bottom = ges + jnp.where(low, -he, he)
    at_r, at_i = lane == 0, lane == half
    top = top + jnp.where(at_r, fix_r, jnp.where(at_i, fix_i, 0.0))
    bottom = bottom + jnp.where(at_r, -fix_i, jnp.where(at_i, fix_r, 0.0))
    stacked = jnp.concatenate([top.astype(jnp.bfloat16), bottom.astype(jnp.bfloat16)], axis=0)
    v = jnp.dot(cs_ref[...], stacked, preferred_element_type=jnp.float32).astype(jnp.bfloat16)
    return jnp.dot(v, col_ref[...], preferred_element_type=jnp.float32)


def accumulate(corr, peak_ref, total_ref, square_ref):
    peak_ref[...] = jnp.maximum(peak_ref[...], corr)
    total_ref[...] += corr
    square_ref[...] += corr * corr


def clear(peak_ref, total_ref, square_ref):
    peak_ref[...] = jnp.full(peak_ref.shape, -3.0e38, jnp.float32)
    total_ref[...] = jnp.zeros(total_ref.shape, jnp.float32)
    square_ref[...] = jnp.zeros(square_ref.shape, jnp.float32)


def search_kernel(e_ref, *refs):
    @pl.when(pl.program_id(0) == 0)
    def _():
        clear(*refs[6:])

    edge = refs[0].shape[0]
    e = e_ref[...].reshape(edge, edge).astype(jnp.float32)
    accumulate(correlate(e, *refs[:6]), *refs[6:])


def remote_kernel(groups, mics, e_ref, *refs):
    operands, maps = refs[:6], refs[6:9]
    full, up_sem, down_sem, side_sem, near_sem, far_sem = refs[9:]
    edge = operands[0].shape[0]
    depth = mics // 2
    per = e_ref.shape[0] // groups
    me = lax.axis_index("mic")
    z, x = me // 2, me % 2
    above, below, beside = me + 2, me - 2, z * 2 + 1 - x
    has_above, has_below = z < depth - 1, z > 0
    mesh_id = pl.DeviceIdType.MESH
    barrier = pltpu.get_barrier_semaphore()

    @pl.when(has_above)
    def _():
        pl.semaphore_signal(barrier, inc=1, device_id={"mic": above}, device_id_type=mesh_id)

    @pl.when(has_below)
    def _():
        pl.semaphore_signal(barrier, inc=1, device_id={"mic": below}, device_id_type=mesh_id)

    pl.semaphore_signal(barrier, inc=1, device_id={"mic": beside}, device_id_type=mesh_id)
    full[me] = e_ref[...]
    clear(*maps)

    peers = 1 + has_above.astype(jnp.int32) + has_below.astype(jnp.int32)
    pl.semaphore_wait(barrier, peers)

    def copy(group, source, column, send_sem, recv_sem, target):
        piece = full.at[source * 2 + column, pl.ds(group * per, per)]
        slot = group * depth + source
        return pltpu.make_async_remote_copy(
            src_ref=piece,
            dst_ref=piece,
            send_sem=send_sem.at[slot],
            recv_sem=recv_sem.at[slot],
            device_id={"mic": target},
            device_id_type=mesh_id,
        )

    go_up = lambda g, source: copy(g, source, x, up_sem, near_sem, above)
    go_down = lambda g, source: copy(g, source, x, down_sem, near_sem, below)
    go_side = lambda g, source: copy(g, source, x, side_sem, far_sem, beside)
    from_side = lambda g, source: copy(g, source, 1 - x, side_sem, far_sem, beside)

    for step in range(groups + depth):
        for hop in range(depth):
            g = step - hop
            if g < 0 or g >= groups:
                continue
            if hop == 0:

                @pl.when(has_above)
                def _(g=g):
                    go_up(g, z).start()

                @pl.when(has_below)
                def _(g=g):
                    go_down(g, z).start()

                go_side(g, z).start()
                continue

            @pl.when(z - hop >= 0)
            def _(g=g, hop=hop):
                go_up(g, z - hop).wait_recv()

                @pl.when(has_above)
                def _():
                    go_up(g, z - hop).start()

                go_side(g, z - hop).start()

            @pl.when(z + hop < depth)
            def _(g=g, hop=hop):
                go_down(g, z + hop).wait_recv()

                @pl.when(has_below)
                def _():
                    go_down(g, z + hop).start()

                go_side(g, z + hop).start()

        g = step - depth
        if g >= 0:
            for source in range(depth):
                from_side(g, source).wait_recv()

            def one(t, carry):
                e = full[:, t].reshape(edge, edge).astype(jnp.float32)
                accumulate(correlate(e, *operands), *maps)
                return carry

            lax.fori_loop(g * per, (g + 1) * per, one, 0)

    for g in range(groups):
        for source in range(depth):
            go_side(g, source).wait_send()

            @pl.when(jnp.logical_and(has_above, z >= source))
            def _(g=g, source=source):
                go_up(g, source).wait_send()

            @pl.when(jnp.logical_and(has_below, z <= source))
            def _(g=g, source=source):
                go_down(g, source).wait_send()


def search_maps(folded, gr, gi, gb, cs, col):
    count, rows, edge = folded.shape
    mics = lax.axis_size("mic")
    place = lambda axis: lax.broadcasted_iota(jnp.int32, (edge, edge), axis)
    flip = ((place(0) + place(1)) % edge == 0).astype(jnp.bfloat16)
    whole = lambda a: pl.BlockSpec(a.shape, lambda t: (0, 0))
    out = jax.ShapeDtypeStruct((edge, edge), jnp.float32)
    cost = pl.CostEstimate(
        flops=count * 350000000, bytes_accessed=count * 600000, transcendentals=0
    )
    if rows % 16 == 0 and mics % 2 == 0:
        groups = GROUPS if count % GROUPS == 0 else 1
        slots = groups * (mics // 2)
        vmem = pl.BlockSpec(memory_space=pltpu.VMEM)
        return pl.pallas_call(
            functools.partial(remote_kernel, groups, mics),
            in_specs=[vmem] * 7,
            out_specs=[vmem] * 3,
            out_shape=[out] * 3,
            scratch_shapes=[pltpu.VMEM((mics, count, rows, edge), jnp.bfloat16)]
            + [pltpu.SemaphoreType.DMA((slots,))] * 5,
            compiler_params=pltpu.CompilerParams(
                vmem_limit_bytes=40 * 1024 * 1024, collective_id=0, has_side_effects=True
            ),
            cost_estimate=cost,
        )(folded, gr, gi, gb, cs, col, flip)
    gathered = lax.all_gather(folded, "mic", axis=1, tiled=True)[None]
    return pl.pallas_call(
        search_kernel,
        grid=(count,),
        in_specs=[pl.BlockSpec((1, 1, edge, edge), lambda t: (0, t, 0, 0))]
        + [whole(a) for a in (gr, gi, gb, cs, col, flip)],
        out_specs=[pl.BlockSpec((edge, edge), lambda t: (0, 0))] * 3,
        out_shape=[out] * 3,
        compiler_params=pltpu.CompilerParams(vmem_limit_bytes=40 * 1024 * 1024),
        cost_estimate=cost,
    )(gathered, gr, gi, gb, cs, col, flip)


def refine_kernel(lib_ref, ctf_ref, g_ref, cs_ref, wanted_ref, out_ref):
    step = pl.program_id(0)
    edge = ctf_ref.shape[0]

    @pl.when(step == 0)
    def _():
        out_ref[...] = jnp.full((edge, edge), -3.0e38, jnp.float32)

    @pl.when(wanted_ref[step] > 0)
    def _():
        gain = ctf_ref[...]
        fr = (lib_ref[0, :, :edge].astype(jnp.float32) * gain).astype(jnp.bfloat16).astype(jnp.float32)
        fi = (lib_ref[0, :, edge:].astype(jnp.float32) * gain).astype(jnp.bfloat16).astype(jnp.float32)
        gr = g_ref[:, :edge].astype(jnp.float32)
        gi = g_ref[:, edge:].astype(jnp.float32)
        zr = (gr * fr + gi * fi).astype(jnp.bfloat16)
        zi = (gi * fr - gr * fi).astype(jnp.bfloat16)
        ci, si = cs_ref[:, :edge], cs_ref[:, edge:]
        dot = lambda a, b: jnp.dot(a, b, preferred_element_type=jnp.float32)
        ur = (dot(ci, zr) - dot(si, zi)).astype(jnp.bfloat16)
        ui = (dot(si, zr) + dot(ci, zi)).astype(jnp.bfloat16)
        corr = dot(ur, ci) - dot(ui, si)
        out_ref[...] = jnp.maximum(out_ref[...], corr)


def refine_map(library, ctf, spectrum, cs, wanted):
    count, edge, width = library.shape
    whole = lambda a: pl.BlockSpec(a.shape, lambda t: (0, 0))
    return pl.pallas_call(
        refine_kernel,
        grid=(count,),
        in_specs=[pl.BlockSpec((1, edge, width), lambda t: (t, 0, 0))]
        + [whole(a) for a in (ctf, spectrum, cs)]
        + [pl.BlockSpec(memory_space=pltpu.SMEM)],
        out_specs=pl.BlockSpec((edge, edge), lambda t: (0, 0)),
        out_shape=jax.ShapeDtypeStruct((edge, edge), jnp.float32),
        compiler_params=pltpu.CompilerParams(vmem_limit_bytes=40 * 1024 * 1024),
        cost_estimate=pl.CostEstimate(flops=count * 700000000, bytes_accessed=count * 1200000, transcendentals=0),
    )(library, ctf, spectrum, cs, wanted)


def join(left, right):
    low = jnp.maximum(left[0], right[0].astype(jnp.float32))
    total = left[1] + right[1].astype(jnp.float32)
    square = left[2] + right[2].astype(jnp.float32)
    return (low, total, square, jnp.maximum(left[3], right[3].astype(jnp.float32)))


def merge(maps):
    size = lax.axis_size("orient")
    edge = maps[0].shape[0]
    half = edge // 2
    core = lax.axis_index("orient") % 2
    near = [(i, i ^ 1) for i in range(size)]
    narrow = lambda values: [a.astype(jnp.bfloat16) for a in values]
    mine = [lax.dynamic_slice_in_dim(a, core * half, half, 0) for a in maps]
    theirs = narrow(lax.dynamic_slice_in_dim(a, (1 - core) * half, half, 0) for a in maps)
    state = join(mine, lax.ppermute(jnp.stack(theirs), "orient", near))
    distance = 2
    while distance < size:
        far = [(i, i ^ distance) for i in range(size)]
        state = join(state, lax.ppermute(jnp.stack(narrow(state)), "orient", far))
        distance *= 2
    final = jnp.stack(narrow(state))
    other = lax.ppermute(final, "orient", near)
    first = jnp.where(core == 0, final, other)
    second = jnp.where(core == 0, other, final)
    return [jnp.concatenate([first[i], second[i]], 0).astype(jnp.float32) for i in range(4)]


def body(micrograph, search_spectra, refine_spectra, ctf, ref_owner, ref_slot):
    edge = micrograph.shape[1]
    half = edge // 2
    fwd_cos, fwd_sin, inv_cos, inv_sin = make_tables(edge)
    ctf_gain = jnp.concatenate([ctf, ctf], 1)
    rows_owned = search_spectra.shape[1]
    first_row = lax.axis_index("mic") * rows_owned
    own_gain = lax.dynamic_slice_in_dim(ctf_gain, first_row, rows_owned, 0)
    filtered = (search_spectra.astype(jnp.float32) * own_gain).astype(jnp.bfloat16)
    folded = fold_half(filtered)
    spectrum = forward(micrograph, fwd_cos, fwd_sin)

    library = refine_spectra[0]
    block_size = library.shape[0]
    ids = lax.all_gather(ref_owner[:, 0] * block_size + ref_slot[:, 0], "orient", axis=0, tiled=True)
    slots = lax.axis_index("orient") * block_size + jnp.arange(block_size, dtype=jnp.int32)
    wanted = jnp.any(slots[:, None] == ids[None, :], axis=1).astype(jnp.int32)
    cs = jnp.asarray(np.concatenate([inv_cos, inv_sin], 1))
    refined = refine_map(library, ctf, spectrum, cs, wanted)

    spec = spectrum.astype(jnp.float32)
    g_r, g_i = spec[:, :edge], spec[:, edge:]
    dc = jnp.stack([g_r[:, 0], g_i[:, 0]], 1)
    ny = jnp.stack([g_r[:, half], g_i[:, half]], 1)
    ga = (dc - ny) * 0.5
    gb = (dc + ny) * 0.5
    lane = lax.broadcasted_iota(jnp.int32, (edge, half), 1)
    h_r = jnp.where(lane == 0, ga[:, 0:1], g_r[:, :half])
    h_i = jnp.where(lane == 0, ga[:, 1:2], g_i[:, :half])
    gr = jnp.concatenate([h_r, h_r], 1)
    gi = jnp.concatenate([h_i, h_i], 1)
    sin_rows = -inv_sin[:half]
    sin_rows[0] = inv_cos[half]
    col = jnp.asarray(np.concatenate([inv_cos[:half], sin_rows], 0))
    peak, total, square = search_maps(folded, gr, gi, gb, cs, col)
    peak, total, square, refined = merge([peak, total, square, refined])
    count = float(lax.axis_size("orient") * search_spectra.shape[0])
    return (peak, total / count, peak * lax.rsqrt(square / count + 1e-05), refined)


def solution(mesh):
    in_specs = (
        P("mic", None),
        P("orient", "mic", None),
        P("mic", "orient", None, None),
        P(),
        P(("mic", "orient"), None),
        P(("mic", "orient"), None),
    )
    out_specs = (P("mic", None), P("mic", None), P("mic", None), P("mic", None))
    return jax.shard_map(body, mesh=mesh, in_specs=in_specs, out_specs=out_specs, check_vma=False)
```

time: 186 us -> 127 us (0.68)
  waiting for transfers between devices: 89.2 us -> 18.1 us
  Pallas kernels: 31.4 us -> 73.3 us
  other arithmetic: 20.7 us -> 6.75 us
  between operations: 15.2 us -> 1.78 us
  local copies, waits for them, and re-layouts: 10.8 us -> 5.2 us
  matrix products: 5.37 us -> 7.99 us
    all_gather x1 -> x0, waiting for transfers between devices: 58.3 us -> none  [gather_half(): return lax.all_gather(folded, 'mic', axis=0)]
    pallas_call x1, Pallas kernels: 26.4 us -> 66.9 us  [search_maps(): pl.pallas_call(functools.partial(remote_kernel, groups, mics), in_specs=[...]
    ppermute x2, waiting for transfers between devices: 12.8 us -> 0.01 us  [the longest x1 0.01 us: fold_half(): lax.ppermute(mirrored[:, 0, :], 'mic', [(m, (mics - m) % mics) for m in r...]
    convert_element_type x5 -> x2, other arithmetic: 8.56 us -> 0.29 us  [the longest x1 0.29 us: search_maps(): flip = ((place(0) + place(1)) % edge == 0).astype(jnp.bfloat16)]
    neg x2 -> x1, other arithmetic: 4.66 us -> 0.08 us  [forward(): -ar]
    unnamed x39 -> x33, local copies, waits for them, and re-layouts: 9.12 us -> 4.56 us
    dot_general x5 -> x6, matrix products: 5.37 us -> 7.99 us  [the longest x1 2.21 us: fold_half(): jnp.einsum('tkc,cl->tkl', filtered, mirror_map, preferred_element_type=jn...]
  transfers between devices with their start and end apart: 6 -> 5, of which waited for: 5 -> 3; matrix products, arithmetic and copies ran while one was open for 10% -> 4% of each run, Pallas kernels for 3% -> 5%
where the time goes in v2:
time: 127 us; the launch traced here: 126 us
  Pallas kernels  73.3 us (58%)
  waiting for transfers between devices  18.1 us (14%)
  starting transfers between devices  8.3 us (7%)
  matrix products  7.99 us (6%)
  other arithmetic  6.75 us (5%)
  local copies, waits for them, and re-layouts  5.2 us (4%)
  blocking collectives  4.89 us (4%)
  between operations  1.78 us (1%)
    pallas_call x1, Pallas kernels, search_maps(): pl.pallas_call(functools.partial(remote_kernel, groups, mics), in_specs=[...  66.9 us
    ppermute x1, waiting for transfers between devices, merge(): state = join(state, lax.ppermute(jnp.stack(narrow(state)), 'orient', far))  13.9 us
    pallas_call x1, Pallas kernels, refine_map(): pl.pallas_call(refine_kernel, grid=(count,), in_specs=[pl.BlockSpec((1, e...  6.46 us
    ppermute x1, starting transfers between devices, fold_half(): rest = lax.ppermute(turned, 'mic', [(m, mics - 1 - m) for m in range(mics)])  6.01 us
    unnamed x1, blocking collectives  4.89 us
    unnamed x33, local copies, waits for them, and re-layouts  4.56 us
  transfers between devices with their start and end apart: 5, of which 3 were waited for; matrix products, arithmetic and copies ran while one was open for 4% of the time, Pallas kernels for 5%

profile of v2, /device:TPU:0, one launch (start us, length us, event | category | flops | bytes accessed | tf_op | source)
XLA Modules:
  0.0 126.3 jit_solution(1823027526619102749)
XLA Ops:
  0.7 1.0 fusion.51
  1.6 2.2 %convolution_convert_fusion.2 = bf16[16,48,384]{2,1,0:T(8,128)(2,1)S(1)} fusion(bf16[768,384,1]{1,0,2:T(8,128)(2,1)} %constant.93, bf16[16,48,768]{2,1,0:T(8,128)(2,1)} %param.12, f32[48,768]{1,0:T(8,128)S(1)} %fusion.51), kind=kOutput, calls=%fused_computation.5 | convolution fusion | flops 455049216 | bytes 2506752 | tf_op jit(solution)/shard_map/tkc,cl->tkl/dot_general | solution.py:61
  3.9 1.1 fusion.2
  5.0 6.0 %collective-permute-start.1 = (bf16[16,48,384]{2,1,0:T(8,128)(2,1)}, bf16[16,48,384]{2,1,0:T(8,128)(2,1)}, u32[]{:S(2)}, u32[]{:S(2)}) collective-permute-start(bf16[16,48,384]{2,1,0:T(8,128)(2,1)} %fusion.2), channel_id=1, source_target_pairs={{0,28},{4,24},{8,20},{12,16},{16,12},{20,8},{24,4},{28,0},{1,29},{... | collective-permute-start | bytes 1769480 | tf_op jit(solution)/shard_map/ppermute | solution.py:71
  11.0 0.7 collective-permute-start
  11.8 0.3 fusion.27.refs_5_
  12.1 0.6 fusion.3
  12.8 0.3 copy-done.8
  13.1 0.5 fusion.8
  13.6 0.2 copy-done.9
  13.7 1.6 %fusion.61 = (f32[384,768]{1,0:T(8,128)}, bf16[384,768]{1,0:T(8,128)(2,1)S(1)}) fusion(f32[768,384]{0,1:T(8,128)S(1)} %fusion.8, bf16[384,384]{1,0:T(8,128)(2,1)S(1)} %copy-done.9, bf16[384,384]{0,1:T(8,128)(2,1)S(1)} %get-tuple-element.40, bf16[384,384]{0,1:T(8,128)(2,1)S(1)} %get-tuple-element.41), kind=kOutput, calls=%fused_computation.133 | convolution fusion | flops 228556800 | bytes 3833856 | tf_op jit(solution)/shard_map/dot_general | solution.py:36
  15.5 0.2 add_multiply_fusion
  15.7 0.3 slice_reduce_fusion
  16.1 0.6 dynamic-slice
  17.5 4.9 %all-reduce = s32[16]{0:T(128)S(1)} all-reduce(s32[16]{0:T(128)S(1)} %bitcast_dynamic-update-slice_fusion), channel_id=2, replica_groups=mesh['mic'=8,'orient'=4] {'orient'}, use_global_device_ids=true, to_apply=%add | all-reduce | flops 16 | bytes 128
  22.3 0.2 compare_reduce_fusion
  22.6 2.3 %copy-done.2 = bf16[1,8,384,768]{3,2,1,0:T(8,128)(2,1)S(1)} copy-done((bf16[1,8,384,768]{3,2,1,0:T(8,128)(2,1)S(1)}, bf16[1,8,384,768]{3,2,1,0:T(8,128)(2,1)}, u32[]{:S(2)}) %copy-start.2) | copy-done | bytes 4718616
  24.9 6.5 %shard_map.139 = f32[384,384]{1,0:T(8,128)S(1)} custom-call(bf16[8,384,768]{2,1,0:T(8,128)(2,1)S(1)} %bitcast.115, f32[384,384]{1,0:T(8,128)S(1)} %copy-done.1, bf16[384,768]{1,0:T(8,128)(2,1)S(1)} %get-tuple-element.44.g_ref, bf16[384,768]{1,0:T(8,128)(2,1)S(1)} %copy-done.3, s32[8]{0:T(128)S(1)} %convert_element_type.158.wanted_ref), custom_call_target="tpu_custom_call" | custom-call | flops 5600000000 | bytes 9600000 | tf_op jit(solution)/shard_map/pallas_call | solution.py:305
  31.4 0.2 slice_select_fusion
  31.6 0.3 pad_maximum_fusion
  31.9 0.9 copy-done.13
  32.9 2.1 %add_convert_fusion.e_ref = bf16[16,48,384]{2,1,0:T(8,128)(2,1)S(1)} fusion(bf16[16,48,384]{2,1,0:T(8,128)(2,1)} %collective-permute-done.1, f32[16,384]{1,0:T(8,128)S(1)} %convert_element_type.145, bf16[16,48,768]{2,1,0:T(8,128)(2,1)S(1)} %copy-done.13, f32[48,768]{1,0:T(8,128)S(1)} %fusion.51, s32[384]{0:T(512)S(1)} %iota_add_fusion, ...), kind=kOutput, calls=%fused_computation.11 | convolution fusion | flops 457703424 | bytes 2537904 | tf_op jit(solution)/shard_map/tkc,cl->tkl/dot_general | solution.py:72
  35.0 66.9 %shard_map.138 = (f32[384,384]{1,0:T(8,128)S(1)}, f32[384,384]{1,0:T(8,128)S(1)}, f32[384,384]{1,0:T(8,128)S(1)}) custom-call(bf16[16,48,384]{2,1,0:T(8,128)(2,1)S(1)} %add_convert_fusion.e_ref, f32[384,384]{1,0:T(8,128)S(1)} %get-tuple-element.49.refs_0_, f32[384,384]{1,0:T(8,128)S(1)} %get-tuple-element.50.refs_1_, ...), custom_call_target="tpu_custom_call" | custom-call | flops 5600000000 | bytes 9600000 | tf_op jit(solution)/shard_map/pallas_call | solution.py:252
  102.0 0.9 pad_maximum_fusion.2
  102.9 2.2 %collective-permute-done.2 = bf16[4,192,384]{2,1,0:T(8,128)(2,1)S(1)} collective-permute-done((bf16[4,192,384]{2,1,0:T(8,128)(2,1)}, bf16[4,192,384]{2,1,0:T(8,128)(2,1)S(1)}, u32[]{:S(2)}, u32[]{:S(2)}) %collective-permute-start.2) | collective-permute-done | bytes 589856 | tf_op jit(solution)/shard_map/ppermute | solution.py:334
  105.3 1.6 %collective-permute-start.3 = (bf16[4,192,384]{2,1,0:T(8,128)(2,1)S(1)}, bf16[4,192,384]{2,1,0:T(8,128)(2,1)S(1)}, u32[]{:S(2)}, u32[]{:S(2)}) collective-permute-start(bf16[4,192,384]{2,1,0:T(8,128)(2,1)S(1)} %pad_maximum_fusion.3), channel_id=1, source_target_pairs={{0,2},{1,3},{2,0},{3,1},{4,6},{5,7},{6,4},{7,5},{8,10},{9,11},{10,... | collective-permute-start | bytes 1769480 | tf_op jit(solution)/shard_map/ppermute | solution.py:338
  106.9 13.9 %collective-permute-done.3 = bf16[4,192,384]{2,1,0:T(8,128)(2,1)S(1)} collective-permute-done((bf16[4,192,384]{2,1,0:T(8,128)(2,1)S(1)}, bf16[4,192,384]{2,1,0:T(8,128)(2,1)S(1)}, u32[]{:S(2)}, u32[]{:S(2)}) %collective-permute-start.3) | collective-permute-done | bytes 589856 | tf_op jit(solution)/shard_map/ppermute | solution.py:338
  121.2 2.0 %collective-permute-done.4 = bf16[4,192,384]{2,1,0:T(8,128)(2,1)S(1)} collective-permute-done((bf16[4,192,384]{2,1,0:T(8,128)(2,1)S(1)}, bf16[4,192,384]{2,1,0:T(8,128)(2,1)S(1)}, u32[]{:S(2)}, u32[]{:S(2)}) %collective-permute-start.4) | collective-permute-done | bytes 589856 | tf_op jit(solution)/shard_map/ppermute | solution.py:341
  123.2 0.2 broadcast_select_fusion.1
  123.5 0.9 maximum_convert_fusion.1
  124.3 0.9 convert_multiply_fusion
  125.2 1.1 rsqrt_multiply_fusion
  (58 shorter events, 1.5 us)
Async XLA Ops:
  0.6 11.4 %copy-start = (bf16[384,384]{1,0:T(8,128)(2,1)S(1)}, bf16[384,384]{1,0:T(8,128)(2,1)}, u32[]{:S(2)}) copy-start(bf16[384,384]{1,0:T(8,128)(2,1)} %param.11) | copy-start | bytes 884740
  1.6 2.2 %copy-start.10 = (bf16[48,48,1]{1,0,2:T(8,128)(2,1)S(1)}, bf16[48,48,1]{1,0,2:T(8,128)(2,1)}, u32[]{:S(2)}) copy-start(bf16[48,48,1]{1,0,2:T(8,128)(2,1)} %constant.94) | copy-start | bytes 13828
  3.9 8.2 %copy-start.7 = (bf16[384,768]{1,0:T(8,128)(2,1)S(1)}, bf16[384,768]{1,0:T(8,128)(2,1)}, u32[]{:S(2)}) copy-start(bf16[384,768]{1,0:T(8,128)(2,1)} %constant.79.clone) | copy-start | bytes 1769476
  5.0 26.9 %collective-permute-start.1 = (bf16[16,48,384]{2,1,0:T(8,128)(2,1)}, bf16[16,48,384]{2,1,0:T(8,128)(2,1)}, u32[]{:S(2)}, u32[]{:S(2)}) collective-permute-start(bf16[16,48,384]{2,1,0:T(8,128)(2,1)} %fusion.2), channel_id=1, source_target_pairs={{0,28},{4,24},{8,20},{12,16},{16,12},{20,8},{24,4},{28,0},{1,29},{... | collective-permute-start | bytes 1769480 | tf_op jit(solution)/shard_map/ppermute | solution.py:71
  11.0 20.9 %collective-permute-start = (bf16[16,384]{1,0:T(8,128)(2,1)S(1)}, bf16[16,384]{1,0:T(8,128)(2,1)S(1)}, u32[]{:S(2)}, u32[]{:S(2)}) collective-permute-start(bf16[16,384]{1,0:T(8,128)(2,1)S(1)} %bitcast.116), channel_id=1, source_target_pairs={{0,0},{4,28},{8,24},{12,20},{16,16},{20,12},{24,8},{28,4},{1,1},{5... | collective-permute-start | bytes 36872 | tf_op jit(solution)/shard_map/ppermute | solution.py:70
  12.1 1.0 copy-start.8
  12.8 1.0 copy-start.9
  15.4 0.7 copy-start.14
  15.4 1.9 %copy-start.11 = (s32[4,1]{0,1:T(1,128)S(1)}, s32[4,1]{0,1:T(1,128)}, u32[]{:S(2)}) copy-start(s32[4,1]{0,1:T(1,128)} %param.16) | copy-start | bytes 52
  15.5 1.9 %copy-start.12 = (s32[4,1]{0,1:T(1,128)S(1)}, s32[4,1]{0,1:T(1,128)}, u32[]{:S(2)}) copy-start(s32[4,1]{0,1:T(1,128)} %param.15) | copy-start | bytes 52
  15.5 7.1 %copy-start.1 = (f32[384,384]{1,0:T(8,128)S(1)}, f32[384,384]{1,0:T(8,128)}, u32[]{:S(2)}) copy-start(f32[384,384]{1,0:T(8,128)} %ctf_ref.1) | copy-start | bytes 1769476
  15.5 7.1 %copy-start.3 = (bf16[384,768]{1,0:T(8,128)(2,1)S(1)}, bf16[384,768]{1,0:T(8,128)(2,1)}, u32[]{:S(2)}) copy-start(bf16[384,768]{1,0:T(8,128)(2,1)} %constant.80.clone.refs_3_.cs_ref) | copy-start | bytes 1769476
  22.6 2.3 %copy-start.2 = (bf16[1,8,384,768]{3,2,1,0:T(8,128)(2,1)S(1)}, bf16[1,8,384,768]{3,2,1,0:T(8,128)(2,1)}, u32[]{:S(2)}) copy-start(bf16[1,8,384,768]{3,2,1,0:T(8,128)(2,1)} %param.13) | copy-start | bytes 14155780
  24.9 6.5 %copy-start.6 = (f32[384,768]{1,0:T(8,128)S(1)}, f32[384,768]{1,0:T(8,128)}, u32[]{:S(2)}) copy-start(f32[384,768]{1,0:T(8,128)} %get-tuple-element.43) | copy-start | bytes 3538948
  31.6 1.3 %copy-start.13 = (bf16[16,48,768]{2,1,0:T(8,128)(2,1)S(1)}, bf16[16,48,768]{2,1,0:T(8,128)(2,1)}, u32[]{:S(2)}) copy-start(bf16[16,48,768]{2,1,0:T(8,128)(2,1)} %param.12) | copy-start | bytes 3538948
  32.9 2.1 %copy-start.4 = (bf16[384,768]{1,0:T(8,128)(2,1)S(1)}, bf16[384,768]{1,0:T(8,128)(2,1)}, u32[]{:S(2)}) copy-start(bf16[384,768]{1,0:T(8,128)(2,1)} %constant.80.clone.refs_3_.cs_ref) | copy-start | bytes 1769476
  32.9 2.1 %copy-start.5 = (bf16[384,384]{1,0:T(8,128)(2,1)S(1)}, bf16[384,384]{1,0:T(8,128)(2,1)}, u32[]{:S(2)}) copy-start(bf16[384,384]{1,0:T(8,128)(2,1)} %constant.81.clone.refs_4_) | copy-start | bytes 884740
  102.9 2.2 %collective-permute-start.2 = (bf16[4,192,384]{2,1,0:T(8,128)(2,1)}, bf16[4,192,384]{2,1,0:T(8,128)(2,1)S(1)}, u32[]{:S(2)}, u32[]{:S(2)}) collective-permute-start(bf16[4,192,384]{2,1,0:T(8,128)(2,1)} %pad_maximum_fusion.2), channel_id=1, source_target_pairs={{0,1},{1,0},{2,3},{3,2},{4,5},{5,4},{6,7},{7,6},{8,9},{9,8},{10,11... | collective-permute-start | bytes 1769480 | tf_op jit(solution)/shard_map/ppermute | solution.py:334
  105.3 15.4 %collective-permute-start.3 = (bf16[4,192,384]{2,1,0:T(8,128)(2,1)S(1)}, bf16[4,192,384]{2,1,0:T(8,128)(2,1)S(1)}, u32[]{:S(2)}, u32[]{:S(2)}) collective-permute-start(bf16[4,192,384]{2,1,0:T(8,128)(2,1)S(1)} %pad_maximum_fusion.3), channel_id=1, source_target_pairs={{0,2},{1,3},{2,0},{3,1},{4,6},{5,7},{6,4},{7,5},{8,10},{9,11},{10,... | collective-permute-start | bytes 1769480 | tf_op jit(solution)/shard_map/ppermute | solution.py:338
  121.1 2.1 %collective-permute-start.4 = (bf16[4,192,384]{2,1,0:T(8,128)(2,1)S(1)}, bf16[4,192,384]{2,1,0:T(8,128)(2,1)S(1)}, u32[]{:S(2)}, u32[]{:S(2)}) collective-permute-start(bf16[4,192,384]{2,1,0:T(8,128)(2,1)S(1)} %pad_maximum_fusion.4), channel_id=1, source_target_pairs={{0,1},{1,0},{2,3},{3,2},{4,5},{5,4},{6,7},{7,6},{8,9},{9,8},{10,11... | collective-permute-start | bytes 1769480 | tf_op jit(solution)/shard_map/ppermute | solution.py:341

commit v3 on v2

--- a/solution.py
+++ b/solution.py
@@ -117,6 +117,23 @@
     square_ref[...] = jnp.zeros(square_ref.shape, jnp.float32)
 
 
+def refine_correlation(template, ctf_ref, g_ref, cs_ref):
+    edge = ctf_ref.shape[0]
+    gain = ctf_ref[...]
+    narrow = lambda a: a.astype(jnp.bfloat16)
+    fr = narrow(template[:, :edge].astype(jnp.float32) * gain).astype(jnp.float32)
+    fi = narrow(template[:, edge:].astype(jnp.float32) * gain).astype(jnp.float32)
+    gr = g_ref[:, :edge].astype(jnp.float32)
+    gi = g_ref[:, edge:].astype(jnp.float32)
+    zr = narrow(gr * fr + gi * fi)
+    zi = narrow(gi * fr - gr * fi)
+    ci, si = cs_ref[:, :edge], cs_ref[:, edge:]
+    dot = lambda a, b: jnp.dot(a, b, preferred_element_type=jnp.float32)
+    ur = narrow(dot(ci, zr) - dot(si, zi))
+    ui = narrow(dot(si, zr) + dot(ci, zi))
+    return dot(ur, ci) - dot(ui, si)
+
+
 def search_kernel(e_ref, *refs):
     @pl.when(pl.program_id(0) == 0)
     def _():
@@ -127,9 +144,12 @@
     accumulate(correlate(e, *refs[:6]), *refs[6:])
 
 
-def remote_kernel(groups, mics, e_ref, *refs):
-    operands, maps = refs[:6], refs[6:9]
-    full, up_sem, down_sem, side_sem, near_sem, far_sem = refs[9:]
+def remote_kernel(groups, mics, blocks, e_ref, *refs):
+    operands, refine_refs = refs[:6], refs[6:10]
+    maps, refined_ref = refs[10:13], refs[13]
+    full, shared, up_sem, down_sem, side_sem, near_sem, far_sem, out_sem, in_sem = refs[14:]
+    listed = refine_refs[0].shape[0]
+    block = lax.axis_index("orient")
     edge = operands[0].shape[0]
     depth = mics // 2
     per = e_ref.shape[0] // groups
@@ -149,10 +169,19 @@
         pl.semaphore_signal(barrier, inc=1, device_id={"mic": below}, device_id_type=mesh_id)
 
     pl.semaphore_signal(barrier, inc=1, device_id={"mic": beside}, device_id_type=mesh_id)
+    for turn in range(1, blocks):
+        pl.semaphore_signal(
+            barrier,
+            inc=1,
+            device_id={"orient": (block + turn) % blocks},
+            device_id_type=mesh_id,
+        )
+
     full[me] = e_ref[...]
+    refined_ref[...] = jnp.full(refined_ref.shape, -3.0e38, jnp.float32)
     clear(*maps)
 
-    peers = 1 + has_above.astype(jnp.int32) + has_below.astype(jnp.int32)
+    peers = blocks + has_above.astype(jnp.int32) + has_below.astype(jnp.int32)
     pl.semaphore_wait(barrier, peers)
 
     def copy(group, source, column, send_sem, recv_sem, target):
@@ -172,6 +201,22 @@
     go_side = lambda g, source: copy(g, source, x, side_sem, far_sem, beside)
     from_side = lambda g, source: copy(g, source, 1 - x, side_sem, far_sem, beside)
 
+    def share(turn, owner):
+        return pltpu.make_async_remote_copy(
+            src_ref=shared.at[owner],
+            dst_ref=shared.at[owner],
+            send_sem=out_sem.at[turn - 1],
+            recv_sem=in_sem.at[turn - 1],
+            device_id={"orient": (block + turn) % blocks},
+            device_id_type=mesh_id,
+        )
+
+    def refine_one(j, carry):
+        lib_ref, ctf_ref, g_ref, cap_ref = refine_refs
+        corr = refine_correlation(lib_ref[j], ctf_ref, g_ref, operands[3])
+        refined_ref[...] = jnp.maximum(refined_ref[...], jnp.minimum(corr, cap_ref[j]))
+        return carry
+
     for step in range(groups + depth):
         for hop in range(depth):
             g = step - hop
@@ -210,6 +255,13 @@
 
                 go_side(g, z + hop).start()
 
+        if step < depth:
+            lax.fori_loop(step * listed // depth, (step + 1) * listed // depth, refine_one, 0)
+        if step == depth - 1:
+            shared[block] = refined_ref[...].astype(jnp.bfloat16)
+            for turn in range(1, blocks):
+                share(turn, block).start()
+
         g = step - depth
         if g >= 0:
             for source in range(depth):
@@ -222,6 +274,13 @@
 
             lax.fori_loop(g * per, (g + 1) * per, one, 0)
 
+    for turn in range(1, blocks):
+        owner = (block + blocks - turn) % blocks
+        share(turn, owner).wait_recv()
+        refined_ref[...] = jnp.maximum(refined_ref[...], shared[owner].astype(jnp.float32))
+    for turn in range(1, blocks):
+        share(turn, block).wait_send()
+
     for g in range(groups):
         for source in range(depth):
             go_side(g, source).wait_send()
@@ -235,7 +294,7 @@
                 go_down(g, source).wait_send()
 
 
-def search_maps(folded, gr, gi, gb, cs, col):
+def all_maps(folded, gr, gi, gb, cs, col, library, ctf, spectrum, wanted):
     count, rows, edge = folded.shape
     mics = lax.axis_size("mic")
     place = lambda axis: lax.broadcasted_iota(jnp.int32, (edge, edge), axis)
@@ -248,21 +307,30 @@
     if rows % 16 == 0 and mics % 2 == 0:
         groups = GROUPS if count % GROUPS == 0 else 1
         slots = groups * (mics // 2)
+        blocks = lax.axis_size("orient")
+        cap = jnp.where(wanted > 0, 3.0e38, -3.0e38).astype(jnp.float32)
+        cap = jnp.broadcast_to(cap[:, None, None], (wanted.shape[0], 1, edge))
         vmem = pl.BlockSpec(memory_space=pltpu.VMEM)
-        return pl.pallas_call(
-            functools.partial(remote_kernel, groups, mics),
-            in_specs=[vmem] * 7,
-            out_specs=[vmem] * 3,
-            out_shape=[out] * 3,
-            scratch_shapes=[pltpu.VMEM((mics, count, rows, edge), jnp.bfloat16)]
-            + [pltpu.SemaphoreType.DMA((slots,))] * 5,
+        *maps, refined = pl.pallas_call(
+            functools.partial(remote_kernel, groups, mics, blocks),
+            in_specs=[vmem] * 11,
+            out_specs=[vmem] * 4,
+            out_shape=[out] * 4,
+            scratch_shapes=[
+                pltpu.VMEM((mics, count, rows, edge), jnp.bfloat16),
+                pltpu.VMEM((blocks, edge, edge), jnp.bfloat16),
+            ]
+            + [pltpu.SemaphoreType.DMA((slots,))] * 5
+            + [pltpu.SemaphoreType.DMA((blocks - 1,))] * 2,
             compiler_params=pltpu.CompilerParams(
                 vmem_limit_bytes=40 * 1024 * 1024, collective_id=0, has_side_effects=True
             ),
             cost_estimate=cost,
-        )(folded, gr, gi, gb, cs, col, flip)
+        )(folded, gr, gi, gb, cs, col, flip, library, ctf, spectrum, cap)
+        return merge(maps) + [refined]
+    refined = refine_map(library, ctf, spectrum, cs, wanted)
     gathered = lax.all_gather(folded, "mic", axis=1, tiled=True)[None]
-    return pl.pallas_call(
+    maps = pl.pallas_call(
         search_kernel,
         grid=(count,),
         in_specs=[pl.BlockSpec((1, 1, edge, edge), lambda t: (0, t, 0, 0))]
@@ -272,6 +340,7 @@
         compiler_params=pltpu.CompilerParams(vmem_limit_bytes=40 * 1024 * 1024),
         cost_estimate=cost,
     )(gathered, gr, gi, gb, cs, col, flip)
+    return merge([*maps, refined])
 
 
 def refine_kernel(lib_ref, ctf_ref, g_ref, cs_ref, wanted_ref, out_ref):
@@ -284,18 +353,7 @@
 
     @pl.when(wanted_ref[step] > 0)
     def _():
-        gain = ctf_ref[...]
-        fr = (lib_ref[0, :, :edge].astype(jnp.float32) * gain).astype(jnp.bfloat16).astype(jnp.float32)
-        fi = (lib_ref[0, :, edge:].astype(jnp.float32) * gain).astype(jnp.bfloat16).astype(jnp.float32)
-        gr = g_ref[:, :edge].astype(jnp.float32)
-        gi = g_ref[:, edge:].astype(jnp.float32)
-        zr = (gr * fr + gi * fi).astype(jnp.bfloat16)
-        zi = (gi * fr - gr * fi).astype(jnp.bfloat16)
-        ci, si = cs_ref[:, :edge], cs_ref[:, edge:]
-        dot = lambda a, b: jnp.dot(a, b, preferred_element_type=jnp.float32)
-        ur = (dot(ci, zr) - dot(si, zi)).astype(jnp.bfloat16)
-        ui = (dot(si, zr) + dot(ci, zi)).astype(jnp.bfloat16)
-        corr = dot(ur, ci) - dot(ui, si)
+        corr = refine_correlation(lib_ref[0], ctf_ref, g_ref, cs_ref)
         out_ref[...] = jnp.maximum(out_ref[...], corr)
 
 
@@ -316,10 +374,10 @@
 
 
 def join(left, right):
-    low = jnp.maximum(left[0], right[0].astype(jnp.float32))
-    total = left[1] + right[1].astype(jnp.float32)
-    square = left[2] + right[2].astype(jnp.float32)
-    return (low, total, square, jnp.maximum(left[3], right[3].astype(jnp.float32)))
+    right = [a.astype(jnp.float32) for a in right]
+    return [
+        jnp.maximum(a, b) if i in (0, 3) else a + b for i, (a, b) in enumerate(zip(left, right))
+    ]
 
 
 def merge(maps):
@@ -341,7 +399,7 @@
     other = lax.ppermute(final, "orient", near)
     first = jnp.where(core == 0, final, other)
     second = jnp.where(core == 0, other, final)
-    return [jnp.concatenate([first[i], second[i]], 0).astype(jnp.float32) for i in range(4)]
+    return [jnp.concatenate([first[i], second[i]], 0).astype(jnp.float32) for i in range(len(maps))]
 
 
 def body(micrograph, search_spectra, refine_spectra, ctf, ref_owner, ref_slot):
@@ -362,7 +420,6 @@
     slots = lax.axis_index("orient") * block_size + jnp.arange(block_size, dtype=jnp.int32)
     wanted = jnp.any(slots[:, None] == ids[None, :], axis=1).astype(jnp.int32)
     cs = jnp.asarray(np.concatenate([inv_cos, inv_sin], 1))
-    refined = refine_map(library, ctf, spectrum, cs, wanted)
 
     spec = spectrum.astype(jnp.float32)
     g_r, g_i = spec[:, :edge], spec[:, edge:]
@@ -378,8 +435,9 @@
     sin_rows = -inv_sin[:half]
     sin_rows[0] = inv_cos[half]
     col = jnp.asarray(np.concatenate([inv_cos[:half], sin_rows], 0))
-    peak, total, square = search_maps(folded, gr, gi, gb, cs, col)
-    peak, total, square, refined = merge([peak, total, square, refined])
+    peak, total, square, refined = all_maps(
+        folded, gr, gi, gb, cs, col, library, ctf, spectrum, wanted
+    )
     count = float(lax.axis_size("orient") * search_spectra.shape[0])
     return (peak, total / count, peak * lax.rsqrt(square / count + 1e-05), refined)
 

time: 127 us -> 125 us (0.984)
  waiting for transfers between devices: 18.1 us -> 14 us
  other arithmetic: 6.75 us -> 9.75 us
  Pallas kernels: 73.3 us -> 71.7 us
    ppermute x1, waiting for transfers between devices: 13.9 us -> 10.5 us  [merge(): state = join(state, lax.ppermute(jnp.stack(narrow(state)), 'orient', far))]
    pallas_call x2 -> x1, Pallas kernels: 73.3 us -> 71.7 us  [all_maps(): pl.pallas_call(functools.partial(remote_kernel, groups, mics, blocks), in...]
    unnamed x33 -> x54, local copies, waits for them, and re-layouts: 4.56 us -> 5.25 us
  transfers between devices with their start and end apart: 5 -> 5, of which waited for: 3 -> 3; matrix products, arithmetic and copies ran while one was open for 4% -> 7% of each run, Pallas kernels for 5% -> 0%
where the time goes in v3:
time: 125 us
  Pallas kernels  71.7 us (57%)
  waiting for transfers between devices  14 us (11%)
  other arithmetic  9.75 us (8%)
  starting transfers between devices  9.44 us (8%)
  matrix products  7.05 us (6%)
  local copies, waits for them, and re-layouts  5.89 us (5%)
  blocking collectives  4.93 us (4%)
  between operations  1.93 us (2%)
    pallas_call x1, Pallas kernels, all_maps(): pl.pallas_call(functools.partial(remote_kernel, groups, mics, blocks), in...  71.7 us
    ppermute x1, waiting for transfers between devices, merge(): state = join(state, lax.ppermute(jnp.stack(narrow(state)), 'orient', far))  10.5 us
    ppermute x1, starting transfers between devices, fold_half(): rest = lax.ppermute(turned, 'mic', [(m, mics - 1 - m) for m in range(mics)])  5.97 us
    unnamed x54, local copies, waits for them, and re-layouts  5.25 us
    unnamed x1, blocking collectives  4.93 us
  transfers between devices with their start and end apart: 5, of which 3 were waited for; matrix products, arithmetic and copies ran while one was open for 7% of the time, Pallas kernels for 0%

profile of v3, /device:TPU:0, one launch (start us, length us, event | category | flops | bytes accessed | tf_op | source)
XLA Modules:
  0.0 124.7 jit_solution(8542957740217030019)
XLA Ops:
  0.7 1.0 fusion.46
  1.7 2.3 %convolution_convert_fusion.2 = bf16[16,48,384]{2,1,0:T(8,128)(2,1)S(1)} fusion(bf16[768,384,1]{1,0,2:T(8,128)(2,1)} %constant.98, bf16[16,48,768]{2,1,0:T(8,128)(2,1)} %param.12, f32[48,768]{1,0:T(8,128)S(1)} %fusion.46), kind=kOutput, calls=%fused_computation.5 | convolution fusion | flops 455049216 | bytes 2506752 | tf_op jit(solution)/shard_map/tkc,cl->tkl/dot_general | solution.py:61
  4.0 1.1 fusion.2
  5.1 6.0 %collective-permute-start.1 = (bf16[16,48,384]{2,1,0:T(8,128)(2,1)}, bf16[16,48,384]{2,1,0:T(8,128)(2,1)}, u32[]{:S(2)}, u32[]{:S(2)}) collective-permute-start(bf16[16,48,384]{2,1,0:T(8,128)(2,1)} %fusion.2), channel_id=1, source_target_pairs={{0,28},{4,24},{8,20},{12,16},{16,12},{20,8},{24,4},{28,0},{1,29},{... | collective-permute-start | bytes 1769480 | tf_op jit(solution)/shard_map/ppermute | solution.py:71
  11.1 1.3 %collective-permute-start = (bf16[16,384]{1,0:T(8,128)(2,1)S(1)}, bf16[16,384]{1,0:T(8,128)(2,1)}, u32[]{:S(2)}, u32[]{:S(2)}) collective-permute-start(bf16[16,384]{1,0:T(8,128)(2,1)S(1)} %bitcast.94), channel_id=1, source_target_pairs={{0,0},{4,28},{8,24},{12,20},{16,16},{20,12},{24,8},{28,4},{1,1},{5... | collective-permute-start | bytes 36872 | tf_op jit(solution)/shard_map/ppermute | solution.py:70
  12.3 0.5 iota_compare_fusion.7
  12.8 0.6 fusion.47
  13.4 0.5 iota_compare_fusion.4
  14.0 0.6 iota_add_fusion
  14.5 0.5 iota_compare_fusion.3
  15.1 0.3 fusion.27.refs_5_
  15.4 0.6 fusion.3
  16.0 0.3 copy-done.10
  16.3 0.5 fusion.8
  17.0 0.5 fusion.56
  17.7 0.9 add_multiply_fusion
  18.6 0.3 slice_reduce_fusion
  18.8 0.7 dynamic-slice
  20.3 4.9 %all-reduce = s32[16]{0:T(128)S(1)} all-reduce(s32[16]{0:T(128)S(1)} %bitcast_dynamic-update-slice_fusion), channel_id=2, replica_groups=mesh['mic'=8,'orient'=4] {'orient'}, use_global_device_ids=true, to_apply=%add | all-reduce | flops 16 | bytes 128
  25.7 1.1 pad_maximum_fusion
  26.8 0.7 convert_element_type.125
  27.7 2.1 %add_convert_fusion.e_ref = bf16[16,48,384]{2,1,0:T(8,128)(2,1)S(1)} fusion(bf16[16,48,384]{2,1,0:T(8,128)(2,1)} %collective-permute-done.1, f32[16,384]{1,0:T(8,128)S(1)} %convert_element_type.125, bf16[16,48,768]{2,1,0:T(8,128)(2,1)S(1)} %copy-done.20, f32[48,768]{1,0:T(8,128)S(1)} %copy-done.13, s32[384]{0:T(512)S(1)} %copy-done.16, ...), kind=kOutput, calls=%fused_computation.11 | convolution fusion | flops 457703424 | bytes 2537904 | tf_op jit(solution)/shard_map/tkc,cl->tkl/dot_general | solution.py:72
  30.0 2.3 %copy-done.6 = bf16[1,8,384,768]{3,2,1,0:T(8,128)(2,1)S(1)} copy-done((bf16[1,8,384,768]{3,2,1,0:T(8,128)(2,1)S(1)}, bf16[1,8,384,768]{3,2,1,0:T(8,128)(2,1)}, u32[]{:S(2)}) %copy-start.6) | copy-done | bytes 4718616
  32.3 71.7 %shard_map.138 = (f32[384,384]{1,0:T(8,128)S(1)}, f32[384,384]{1,0:T(8,128)S(1)}, f32[384,384]{1,0:T(8,128)S(1)}, f32[384,384]{1,0:T(8,128)S(1)}) custom-call(bf16[16,48,384]{2,1,0:T(8,128)(2,1)S(1)} %add_convert_fusion.e_ref, f32[384,384]{1,0:T(8,128)S(1)} %get-tuple-element.45.refs_0_, f32[384,384]{1,0:T(8,128)S(1)} %copy-done.2, f32[384,2]{1,0:T(8,128)S(1)} %copy-done.5, ...), custom_call_target="tpu_custom_call" | custom-call | flops 5600000000 | bytes 9600000 | tf_op jit(solution)/shard_map/pallas_call | solution.py:314
  104.0 0.8 copy-done.3
  105.1 1.8 %collective-permute-done.2 = bf16[3,192,384]{2,1,0:T(8,128)(2,1)S(1)} collective-permute-done((bf16[3,192,384]{2,1,0:T(8,128)(2,1)S(1)}, bf16[3,192,384]{2,1,0:T(8,128)(2,1)S(1)}, u32[]{:S(2)}, u32[]{:S(2)}) %collective-permute-start.2) | collective-permute-done | bytes 442400 | tf_op jit(solution)/shard_map/ppermute | solution.py:392
  107.0 2.1 %collective-permute-start.3 = (bf16[3,192,384]{2,1,0:T(8,128)(2,1)S(1)}, bf16[3,192,384]{2,1,0:T(8,128)(2,1)S(1)}, u32[]{:S(2)}, u32[]{:S(2)}) collective-permute-start(bf16[3,192,384]{2,1,0:T(8,128)(2,1)S(1)} %pad_maximum_fusion.3), channel_id=1, source_target_pairs={{0,2},{1,3},{2,0},{3,1},{4,6},{5,7},{6,4},{7,5},{8,10},{9,11},{10,... | collective-permute-start | bytes 1327112 | tf_op jit(solution)/shard_map/ppermute | solution.py:396
  109.1 10.5 %collective-permute-done.3 = bf16[3,192,384]{2,1,0:T(8,128)(2,1)S(1)} collective-permute-done((bf16[3,192,384]{2,1,0:T(8,128)(2,1)S(1)}, bf16[3,192,384]{2,1,0:T(8,128)(2,1)S(1)}, u32[]{:S(2)}, u32[]{:S(2)}) %collective-permute-start.3) | collective-permute-done | bytes 442400 | tf_op jit(solution)/shard_map/ppermute | solution.py:396
  119.9 1.8 %collective-permute-done.4 = bf16[3,192,384]{2,1,0:T(8,128)(2,1)S(1)} collective-permute-done((bf16[3,192,384]{2,1,0:T(8,128)(2,1)S(1)}, bf16[3,192,384]{2,1,0:T(8,128)(2,1)S(1)}, u32[]{:S(2)}, u32[]{:S(2)}) %collective-permute-start.4) | collective-permute-done | bytes 442400 | tf_op jit(solution)/shard_map/ppermute | solution.py:399
  121.9 0.9 convert_multiply_fusion
  122.8 1.1 rsqrt_multiply_fusion
  123.9 0.8 copy.38
  (77 shorter events, 2.0 us)
Async XLA Ops:
  0.6 14.7 %copy-start = (bf16[384,384]{1,0:T(8,128)(2,1)S(1)}, bf16[384,384]{1,0:T(8,128)(2,1)}, u32[]{:S(2)}) copy-start(bf16[384,384]{1,0:T(8,128)(2,1)} %param.11) | copy-start | bytes 884740
  1.6 2.3 %copy-start.12 = (f32[48,768]{1,0:T(8,128)}, f32[48,768]{1,0:T(8,128)S(1)}, u32[]{:S(2)}) copy-start(f32[48,768]{1,0:T(8,128)S(1)} %fusion.46) | copy-start | bytes 442372
  1.6 2.3 %copy-start.14 = (bf16[48,48,1]{1,0,2:T(8,128)(2,1)S(1)}, bf16[48,48,1]{1,0,2:T(8,128)(2,1)}, u32[]{:S(2)}) copy-start(bf16[48,48,1]{1,0,2:T(8,128)(2,1)} %constant.99) | copy-start | bytes 13828
  3.9 11.4 %copy-start.9 = (bf16[384,768]{1,0:T(8,128)(2,1)S(1)}, bf16[384,768]{1,0:T(8,128)(2,1)}, u32[]{:S(2)}) copy-start(bf16[384,768]{1,0:T(8,128)(2,1)} %constant.84.clone) | copy-start | bytes 1769476
  5.1 22.5 %collective-permute-start.1 = (bf16[16,48,384]{2,1,0:T(8,128)(2,1)}, bf16[16,48,384]{2,1,0:T(8,128)(2,1)}, u32[]{:S(2)}, u32[]{:S(2)}) collective-permute-start(bf16[16,48,384]{2,1,0:T(8,128)(2,1)} %fusion.2), channel_id=1, source_target_pairs={{0,28},{4,24},{8,20},{12,16},{16,12},{20,8},{24,4},{28,0},{1,29},{... | collective-permute-start | bytes 1769480 | tf_op jit(solution)/shard_map/ppermute | solution.py:71
  11.1 15.8 %collective-permute-start = (bf16[16,384]{1,0:T(8,128)(2,1)S(1)}, bf16[16,384]{1,0:T(8,128)(2,1)}, u32[]{:S(2)}, u32[]{:S(2)}) collective-permute-start(bf16[16,384]{1,0:T(8,128)(2,1)S(1)} %bitcast.94), channel_id=1, source_target_pairs={{0,0},{4,28},{8,24},{12,20},{16,16},{20,12},{24,8},{28,4},{1,1},{5... | collective-permute-start | bytes 36872 | tf_op jit(solution)/shard_map/ppermute | solution.py:70
  15.4 1.0 copy-start.10
  16.0 1.0 copy-start.11
  17.7 1.2 copy-start.21
  17.7 2.6 %copy-start.18 = (s32[4,1]{0,1:T(1,128)S(1)}, s32[4,1]{0,1:T(1,128)}, u32[]{:S(2)}) copy-start(s32[4,1]{0,1:T(1,128)} %param.16) | copy-start | bytes 52
  17.7 2.5 %copy-start.19 = (s32[4,1]{0,1:T(1,128)S(1)}, s32[4,1]{0,1:T(1,128)}, u32[]{:S(2)}) copy-start(s32[4,1]{0,1:T(1,128)} %param.15) | copy-start | bytes 52
  17.7 7.8 %copy-start.17 = (pred[192]{0:T(512)(128)(4,1)S(1)}, pred[192]{0:T(512)(128)(4,1)}, u32[]{:S(2)}) copy-start(pred[192]{0:T(512)(128)(4,1)} %iota_compare_fusion.7) | copy-start | bytes 580
  25.6 1.9 %copy-start.13 = (f32[48,768]{1,0:T(8,128)S(1)}, f32[48,768]{1,0:T(8,128)}, u32[]{:S(2)}) copy-start(f32[48,768]{1,0:T(8,128)} %copy-done.12) | copy-start | bytes 442372
  25.6 1.9 %copy-start.15 = (bf16[768]{0:T(1024)(128)(2,1)S(1)}, bf16[768]{0:T(1024)(128)(2,1)}, u32[]{:S(2)}) copy-start(bf16[768]{0:T(1024)(128)(2,1)} %get-tuple-element.44) | copy-start | bytes 4612
  25.6 1.9 %copy-start.16 = (s32[384]{0:T(512)S(1)}, s32[384]{0:T(512)}, u32[]{:S(2)}) copy-start(s32[384]{0:T(512)} %iota_add_fusion) | copy-start | bytes 4612
  25.7 1.9 %copy-start.20 = (bf16[16,48,768]{2,1,0:T(8,128)(2,1)S(1)}, bf16[16,48,768]{2,1,0:T(8,128)(2,1)}, u32[]{:S(2)}) copy-start(bf16[16,48,768]{2,1,0:T(8,128)(2,1)} %param.12) | copy-start | bytes 3538948
  25.7 1.9 %copy-start.22 = (pred[768]{0:T(1024)(128)(4,1)S(1)}, pred[768]{0:T(1024)(128)(4,1)}, u32[]{:S(2)}) copy-start(pred[768]{0:T(1024)(128)(4,1)} %iota_compare_fusion.3) | copy-start | bytes 2308
  25.7 1.9 %copy-start.23 = (pred[384]{0:T(512)(128)(4,1)S(1)}, pred[384]{0:T(512)(128)(4,1)}, u32[]{:S(2)}) copy-start(pred[384]{0:T(512)(128)(4,1)} %get-tuple-element.41) | copy-start | bytes 1156
  25.7 1.9 %copy-start.24 = (pred[384]{0:T(512)(128)(4,1)S(1)}, pred[384]{0:T(512)(128)(4,1)}, u32[]{:S(2)}) copy-start(pred[384]{0:T(512)(128)(4,1)} %get-tuple-element.42) | copy-start | bytes 1156
  27.6 2.3 %copy-start.1 = (f32[384,384]{1,0:T(8,128)S(1)}, f32[384,384]{1,0:T(8,128)}, u32[]{:S(2)}) copy-start(f32[384,384]{1,0:T(8,128)} %refs_7_.1) | copy-start | bytes 1769476
  27.6 2.3 %copy-start.2 = (f32[384,384]{1,0:T(8,128)S(1)}, f32[384,384]{1,0:T(8,128)}, u32[]{:S(2)}) copy-start(f32[384,384]{1,0:T(8,128)} %get-tuple-element.46.refs_1_) | copy-start | bytes 1769476
  27.6 2.3 %copy-start.5 = (f32[384,2]{1,0:T(8,128)S(1)}, f32[384,2]{1,0:T(8,128)}, u32[]{:S(2)}) copy-start(f32[384,2]{1,0:T(8,128)} %get-tuple-element.22.refs_2_) | copy-start | bytes 9220
  27.6 2.3 %copy-start.7 = (bf16[384,768]{1,0:T(8,128)(2,1)S(1)}, bf16[384,768]{1,0:T(8,128)(2,1)}, u32[]{:S(2)}) copy-start(bf16[384,768]{1,0:T(8,128)(2,1)} %constant.85.clone.refs_3_) | copy-start | bytes 1769476
  27.7 2.3 %copy-start.8 = (bf16[384,384]{1,0:T(8,128)(2,1)S(1)}, bf16[384,384]{1,0:T(8,128)(2,1)}, u32[]{:S(2)}) copy-start(bf16[384,384]{1,0:T(8,128)(2,1)} %constant.86.clone.refs_4_) | copy-start | bytes 884740
  29.9 2.3 %copy-start.6 = (bf16[1,8,384,768]{3,2,1,0:T(8,128)(2,1)S(1)}, bf16[1,8,384,768]{3,2,1,0:T(8,128)(2,1)}, u32[]{:S(2)}) copy-start(bf16[1,8,384,768]{3,2,1,0:T(8,128)(2,1)} %param.13) | copy-start | bytes 14155780
  104.0 0.8 copy-start.3
  104.8 2.0 %copy-start.4 = (f32[384,384]{1,0:T(8,128)S(1)}, f32[384,384]{1,0:T(8,128)}, u32[]{:S(2)}) copy-start(f32[384,384]{1,0:T(8,128)} %copy-done.3) | copy-start | bytes 1769476
  105.0 1.9 %collective-permute-start.2 = (bf16[3,192,384]{2,1,0:T(8,128)(2,1)S(1)}, bf16[3,192,384]{2,1,0:T(8,128)(2,1)S(1)}, u32[]{:S(2)}, u32[]{:S(2)}) collective-permute-start(bf16[3,192,384]{2,1,0:T(8,128)(2,1)S(1)} %pad_maximum_fusion.2), channel_id=1, source_target_pairs={{0,1},{1,0},{2,3},{3,2},{4,5},{5,4},{6,7},{7,6},{8,9},{9,8},{10,11... | collective-permute-start | bytes 1327112 | tf_op jit(solution)/shard_map/ppermute | solution.py:392
  107.0 12.5 %collective-permute-start.3 = (bf16[3,192,384]{2,1,0:T(8,128)(2,1)S(1)}, bf16[3,192,384]{2,1,0:T(8,128)(2,1)S(1)}, u32[]{:S(2)}, u32[]{:S(2)}) collective-permute-start(bf16[3,192,384]{2,1,0:T(8,128)(2,1)S(1)} %pad_maximum_fusion.3), channel_id=1, source_target_pairs={{0,2},{1,3},{2,0},{3,1},{4,6},{5,7},{6,4},{7,5},{8,10},{9,11},{10,... | collective-permute-start | bytes 1327112 | tf_op jit(solution)/shard_map/ppermute | solution.py:396
  119.8 1.9 %collective-permute-start.4 = (bf16[3,192,384]{2,1,0:T(8,128)(2,1)S(1)}, bf16[3,192,384]{2,1,0:T(8,128)(2,1)S(1)}, u32[]{:S(2)}, u32[]{:S(2)}) collective-permute-start(bf16[3,192,384]{2,1,0:T(8,128)(2,1)S(1)} %pad_maximum_fusion.4), channel_id=1, source_target_pairs={{0,1},{1,0},{2,3},{3,2},{4,5},{5,4},{6,7},{7,6},{8,9},{9,8},{10,11... | collective-permute-start | bytes 1327112 | tf_op jit(solution)/shard_map/ppermute | solution.py:399

commit v4 on v3

--- a/solution.py
+++ b/solution.py
@@ -68,11 +68,10 @@
         "ik,tkl->til", jnp.asarray(flip, jnp.bfloat16), mirrored, preferred_element_type=jnp.float32
     ).astype(jnp.bfloat16)
     first = lax.ppermute(mirrored[:, 0, :], "mic", [(m, (mics - m) % mics) for m in range(mics)])
-    rest = lax.ppermute(turned, "mic", [(m, mics - 1 - m) for m in range(mics)])
     own = jnp.einsum("tkc,cl->tkl", filtered, own_map, preferred_element_type=jnp.float32)
     row = lax.broadcasted_iota(jnp.int32, (1, rows, 1), 1)
-    other = jnp.where(row == 0, first[:, None, :].astype(jnp.float32), rest.astype(jnp.float32))
-    return (own + other).astype(jnp.bfloat16)
+    own = own + jnp.where(row == 0, first[:, None, :].astype(jnp.float32), 0.0)
+    return own.astype(jnp.bfloat16), turned
 
 
 def correlate(e, gr_ref, gi_ref, gb_ref, cs_ref, col_ref, flip_ref):
@@ -144,10 +143,11 @@
     accumulate(correlate(e, *refs[:6]), *refs[6:])
 
 
-def remote_kernel(groups, mics, blocks, e_ref, *refs):
+def remote_kernel(groups, mics, blocks, e_ref, turned_ref, *refs):
     operands, refine_refs = refs[:6], refs[6:10]
     maps, refined_ref = refs[10:13], refs[13]
-    full, shared, up_sem, down_sem, side_sem, near_sem, far_sem, out_sem, in_sem = refs[14:]
+    full, shared, mirror, up_sem, down_sem, side_sem, near_sem, far_sem = refs[14:22]
+    out_sem, in_sem, there_sem, back_sem = refs[22:]
     listed = refine_refs[0].shape[0]
     block = lax.axis_index("orient")
     edge = operands[0].shape[0]
@@ -177,11 +177,12 @@
             device_id_type=mesh_id,
         )
 
-    full[me] = e_ref[...]
+    opposite = mics - 1 - me
+    pl.semaphore_signal(barrier, inc=1, device_id={"mic": opposite}, device_id_type=mesh_id)
     refined_ref[...] = jnp.full(refined_ref.shape, -3.0e38, jnp.float32)
     clear(*maps)
 
-    peers = blocks + has_above.astype(jnp.int32) + has_below.astype(jnp.int32)
+    peers = 1 + blocks + has_above.astype(jnp.int32) + has_below.astype(jnp.int32)
     pl.semaphore_wait(barrier, peers)
 
     def copy(group, source, column, send_sem, recv_sem, target):
@@ -217,12 +218,32 @@
         refined_ref[...] = jnp.maximum(refined_ref[...], jnp.minimum(corr, cap_ref[j]))
         return carry
 
+    def swap(g):
+        rows = pl.ds(g * per, per)
+        return pltpu.make_async_remote_copy(
+            src_ref=turned_ref.at[rows],
+            dst_ref=mirror.at[rows],
+            send_sem=there_sem.at[g],
+            recv_sem=back_sem.at[g],
+            device_id={"mic": opposite},
+            device_id_type=mesh_id,
+        )
+
+    for g in range(min(2, groups)):
+        swap(g).start()
+
     for step in range(groups + depth):
         for hop in range(depth):
             g = step - hop
             if g < 0 or g >= groups:
                 continue
             if hop == 0:
+                swap(g).wait_recv()
+                if g + 2 < groups:
+                    swap(g + 2).start()
+                rows = pl.ds(g * per, per)
+                both = e_ref[rows].astype(jnp.float32) + mirror[rows].astype(jnp.float32)
+                full[me, rows] = both.astype(jnp.bfloat16)
 
                 @pl.when(has_above)
                 def _(g=g):
@@ -280,6 +301,8 @@
         refined_ref[...] = jnp.maximum(refined_ref[...], shared[owner].astype(jnp.float32))
     for turn in range(1, blocks):
         share(turn, block).wait_send()
+    for g in range(groups):
+        swap(g).wait_send()
 
     for g in range(groups):
         for source in range(depth):
@@ -294,7 +317,7 @@
                 go_down(g, source).wait_send()
 
 
-def all_maps(folded, gr, gi, gb, cs, col, library, ctf, spectrum, wanted):
+def all_maps(folded, turned, gr, gi, gb, cs, col, library, ctf, spectrum, wanted):
     count, rows, edge = folded.shape
     mics = lax.axis_size("mic")
     place = lambda axis: lax.broadcasted_iota(jnp.int32, (edge, edge), axis)
@@ -313,22 +336,26 @@
         vmem = pl.BlockSpec(memory_space=pltpu.VMEM)
         *maps, refined = pl.pallas_call(
             functools.partial(remote_kernel, groups, mics, blocks),
-            in_specs=[vmem] * 11,
+            in_specs=[vmem] * 12,
             out_specs=[vmem] * 4,
             out_shape=[out] * 4,
             scratch_shapes=[
                 pltpu.VMEM((mics, count, rows, edge), jnp.bfloat16),
                 pltpu.VMEM((blocks, edge, edge), jnp.bfloat16),
+                pltpu.VMEM((count, rows, edge), jnp.bfloat16),
             ]
             + [pltpu.SemaphoreType.DMA((slots,))] * 5
-            + [pltpu.SemaphoreType.DMA((blocks - 1,))] * 2,
+            + [pltpu.SemaphoreType.DMA((blocks - 1,))] * 2
+            + [pltpu.SemaphoreType.DMA((groups,))] * 2,
             compiler_params=pltpu.CompilerParams(
                 vmem_limit_bytes=40 * 1024 * 1024, collective_id=0, has_side_effects=True
             ),
             cost_estimate=cost,
-        )(folded, gr, gi, gb, cs, col, flip, library, ctf, spectrum, cap)
+        )(folded, turned, gr, gi, gb, cs, col, flip, library, ctf, spectrum, cap)
         return merge(maps) + [refined]
     refined = refine_map(library, ctf, spectrum, cs, wanted)
+    rest = lax.ppermute(turned, "mic", [(m, mics - 1 - m) for m in range(mics)])
+    folded = (folded.astype(jnp.float32) + rest.astype(jnp.float32)).astype(jnp.bfloat16)
     gathered = lax.all_gather(folded, "mic", axis=1, tiled=True)[None]
     maps = pl.pallas_call(
         search_kernel,
@@ -411,7 +438,7 @@
     first_row = lax.axis_index("mic") * rows_owned
     own_gain = lax.dynamic_slice_in_dim(ctf_gain, first_row, rows_owned, 0)
     filtered = (search_spectra.astype(jnp.float32) * own_gain).astype(jnp.bfloat16)
-    folded = fold_half(filtered)
+    folded, turned = fold_half(filtered)
     spectrum = forward(micrograph, fwd_cos, fwd_sin)
 
     library = refine_spectra[0]
@@ -436,7 +463,7 @@
     sin_rows[0] = inv_cos[half]
     col = jnp.asarray(np.concatenate([inv_cos[:half], sin_rows], 0))
     peak, total, square, refined = all_maps(
-        folded, gr, gi, gb, cs, col, library, ctf, spectrum, wanted
+        folded, turned, gr, gi, gb, cs, col, library, ctf, spectrum, wanted
     )
     count = float(lax.axis_size("orient") * search_spectra.shape[0])
     return (peak, total / count, peak * lax.rsqrt(square / count + 1e-05), refined)

time: 125 us -> 139 us (1.11)
  the two profiles are of different devices: /device:TPU:0 before, /device:TPU:19 now
where the time goes in v4:
time: 139 us; the launch traced here: 138 us
  Pallas kernels  87.8 us (63%)
  waiting for transfers between devices  14.2 us (10%)
  other arithmetic  10.8 us (8%)
  starting transfers between devices  6.8 us (5%)
  local copies, waits for them, and re-layouts  6.46 us (5%)
  matrix products  6.06 us (4%)
  blocking collectives  4.52 us (3%)
  between operations  1.81 us (1%)
    pallas_call x1, Pallas kernels, all_maps(): pl.pallas_call(functools.partial(remote_kernel, groups, mics, blocks), in...  87.8 us
    ppermute x1, waiting for transfers between devices, merge(): state = join(state, lax.ppermute(jnp.stack(narrow(state)), 'orient', far))  11.1 us
    unnamed x58, local copies, waits for them, and re-layouts  5.82 us
    unnamed x1, blocking collectives  4.52 us
    ppermute x1, starting transfers between devices, merge(): state = join(mine, lax.ppermute(jnp.stack(theirs), 'orient', near))  3.15 us
  transfers between devices with their start and end apart: 4, of which 3 were waited for; matrix products, arithmetic and copies ran while one was open for 7% of the time, Pallas kernels for 0%

profile of v4, /device:TPU:19, one launch (start us, length us, event | category | flops | bytes accessed | tf_op | source)
XLA Modules:
  0.0 138.5 jit_solution(15374202033459628305)
XLA Ops:
  0.7 1.0 fusion.46
  1.7 2.3 %convolution_convert_fusion.2 = bf16[16,48,384]{2,1,0:T(8,128)(2,1)S(1)} fusion(bf16[768,384,1]{1,0,2:T(8,128)(2,1)} %constant.98, bf16[16,48,768]{2,1,0:T(8,128)(2,1)} %param.12, f32[48,768]{1,0:T(8,128)S(1)} %fusion.46), kind=kOutput, calls=%fused_computation.5 | convolution fusion | flops 455049216 | bytes 2506752 | tf_op jit(solution)/shard_map/tkc,cl->tkl/dot_general | solution.py:61
  4.0 2.1 %collective-permute-start = (bf16[16,384]{1,0:T(8,128)(2,1)S(1)}, bf16[16,384]{1,0:T(8,128)(2,1)}, u32[]{:S(2)}, u32[]{:S(2)}) collective-permute-start(bf16[16,384]{1,0:T(8,128)(2,1)S(1)} %bitcast.94), channel_id=1, source_target_pairs={{0,0},{4,28},{8,24},{12,20},{16,16},{20,12},{24,8},{28,4},{1,1},{5... | collective-permute-start | bytes 36872 | tf_op jit(solution)/shard_map/ppermute | solution.py:70
  6.1 0.5 iota_compare_fusion.7
  6.6 0.5 fusion.47
  7.1 0.6 iota_compare_fusion.4
  7.7 0.6 iota_add_fusion
  8.3 0.6 iota_compare_fusion.3
  8.9 0.3 fusion.27.refs_5_
  9.3 0.6 fusion.3
  9.9 0.3 copy-done.12
  10.2 0.5 fusion.8
  10.9 1.5 %fusion.56 = (f32[384,768]{1,0:T(8,128)}, bf16[384,768]{1,0:T(8,128)(2,1)S(1)}) fusion(f32[768,384]{0,1:T(8,128)S(1)} %fusion.8, bf16[384,384]{1,0:T(8,128)(2,1)S(1)} %copy-done.13, bf16[384,384]{0,1:T(8,128)(2,1)S(1)} %get-tuple-element.28, bf16[384,384]{0,1:T(8,128)(2,1)S(1)} %get-tuple-element.29), kind=kOutput, calls=%fused_computation.121 | convolution fusion | flops 228556800 | bytes 3833856 | tf_op jit(solution)/shard_map/dot_general | solution.py:36
  12.6 0.9 add_multiply_fusion
  14.1 0.6 dynamic-slice
  15.4 4.5 %all-reduce = s32[16]{0:T(128)S(1)} all-reduce(s32[16]{0:T(128)S(1)} %bitcast_dynamic-update-slice_fusion), channel_id=2, replica_groups=mesh['mic'=8,'orient'=4] {'orient'}, use_global_device_ids=true, to_apply=%add | all-reduce | flops 16 | bytes 128
  20.4 1.3 pad_maximum_fusion
  21.7 0.7 convert_element_type.121
  22.5 0.9 add_convert_fusion.e_ref
  24.2 2.3 %copy-done.7 = bf16[1,8,384,768]{3,2,1,0:T(8,128)(2,1)S(1)} copy-done((bf16[1,8,384,768]{3,2,1,0:T(8,128)(2,1)S(1)}, bf16[1,8,384,768]{3,2,1,0:T(8,128)(2,1)}, u32[]{:S(2)}) %copy-start.7) | copy-done | bytes 4718616
  26.6 87.8 %shard_map.138 = (f32[384,384]{1,0:T(8,128)S(1)}, f32[384,384]{1,0:T(8,128)S(1)}, f32[384,384]{1,0:T(8,128)S(1)}, f32[384,384]{1,0:T(8,128)S(1)}) custom-call(bf16[16,48,384]{2,1,0:T(8,128)(2,1)S(1)} %add_convert_fusion.e_ref, bf16[16,48,384]{2,1,0:T(8,128)(2,1)S(1)} %fusion.2.turned_ref, f32[384,384]{1,0:T(8,128)S(1)} %copy-done.2, ...), custom_call_target="tpu_custom_call" | custom-call | flops 5600000000 | bytes 9600000 | tf_op jit(solution)/shard_map/pallas_call | solution.py:337
  114.4 0.8 copy-done.4
  115.3 0.8 pad_maximum_fusion.2
  116.1 3.1 %collective-permute-start.1 = (bf16[3,192,384]{2,1,0:T(8,128)(2,1)}, bf16[3,192,384]{2,1,0:T(8,128)(2,1)S(1)}, u32[]{:S(2)}, u32[]{:S(2)}) collective-permute-start(bf16[3,192,384]{2,1,0:T(8,128)(2,1)} %pad_maximum_fusion.2), channel_id=1, source_target_pairs={{0,1},{1,0},{2,3},{3,2},{4,5},{5,4},{6,7},{7,6},{8,9},{9,8},{10,11... | collective-permute-start | bytes 1327112 | tf_op jit(solution)/shard_map/ppermute | solution.py:419
  119.3 1.6 %collective-permute-done.1 = bf16[3,192,384]{2,1,0:T(8,128)(2,1)S(1)} collective-permute-done((bf16[3,192,384]{2,1,0:T(8,128)(2,1)}, bf16[3,192,384]{2,1,0:T(8,128)(2,1)S(1)}, u32[]{:S(2)}, u32[]{:S(2)}) %collective-permute-start.1) | collective-permute-done | bytes 442400 | tf_op jit(solution)/shard_map/ppermute | solution.py:419
  121.1 0.3 collective-permute-start.2
  121.4 11.1 %collective-permute-done.2 = bf16[3,192,384]{2,1,0:T(8,128)(2,1)S(1)} collective-permute-done((bf16[3,192,384]{2,1,0:T(8,128)(2,1)S(1)}, bf16[3,192,384]{2,1,0:T(8,128)(2,1)S(1)}, u32[]{:S(2)}, u32[]{:S(2)}) %collective-permute-start.2) | collective-permute-done | bytes 442400 | tf_op jit(solution)/shard_map/ppermute | solution.py:423
  132.8 1.3 collective-permute-start.3
  134.1 1.4 %collective-permute-done.3 = bf16[3,192,384]{2,1,0:T(8,128)(2,1)S(1)} collective-permute-done((bf16[3,192,384]{2,1,0:T(8,128)(2,1)S(1)}, bf16[3,192,384]{2,1,0:T(8,128)(2,1)S(1)}, u32[]{:S(2)}, u32[]{:S(2)}) %collective-permute-start.3) | collective-permute-done | bytes 442400 | tf_op jit(solution)/shard_map/ppermute | solution.py:426
  135.7 0.9 convert_multiply_fusion
  136.6 1.1 rsqrt_multiply_fusion
  137.7 0.8 copy.38
  (79 shorter events, 3.0 us)
Async XLA Ops:
  0.6 8.6 %copy-start = (bf16[384,384]{1,0:T(8,128)(2,1)S(1)}, bf16[384,384]{1,0:T(8,128)(2,1)}, u32[]{:S(2)}) copy-start(bf16[384,384]{1,0:T(8,128)(2,1)} %param.11) | copy-start | bytes 884740
  1.6 2.3 %copy-start.14 = (f32[48,768]{1,0:T(8,128)}, f32[48,768]{1,0:T(8,128)S(1)}, u32[]{:S(2)}) copy-start(f32[48,768]{1,0:T(8,128)S(1)} %fusion.46) | copy-start | bytes 442372
  1.6 7.6 %copy-start.11 = (bf16[384,768]{1,0:T(8,128)(2,1)S(1)}, bf16[384,768]{1,0:T(8,128)(2,1)}, u32[]{:S(2)}) copy-start(bf16[384,768]{1,0:T(8,128)(2,1)} %constant.84.clone) | copy-start | bytes 1769476
  4.0 17.7 %collective-permute-start = (bf16[16,384]{1,0:T(8,128)(2,1)S(1)}, bf16[16,384]{1,0:T(8,128)(2,1)}, u32[]{:S(2)}, u32[]{:S(2)}) collective-permute-start(bf16[16,384]{1,0:T(8,128)(2,1)S(1)} %bitcast.94), channel_id=1, source_target_pairs={{0,0},{4,28},{8,24},{12,20},{16,16},{20,12},{24,8},{28,4},{1,1},{5... | collective-permute-start | bytes 36872 | tf_op jit(solution)/shard_map/ppermute | solution.py:70
  9.2 1.0 copy-start.12
  9.9 1.0 copy-start.13
  12.5 1.2 copy-start.16
  12.6 1.5 %copy-start.23 = (u32[32]{0:T(128)S(1)}, u32[32]{0:T(128)}, u32[]{:S(2)}) copy-start(u32[32]{0:T(128)} %constant.94) | copy-start | bytes 388
  12.6 2.7 %copy-start.20 = (s32[4,1]{0,1:T(1,128)S(1)}, s32[4,1]{0,1:T(1,128)}, u32[]{:S(2)}) copy-start(s32[4,1]{0,1:T(1,128)} %param.16) | copy-start | bytes 52
  12.6 2.7 %copy-start.21 = (s32[4,1]{0,1:T(1,128)S(1)}, s32[4,1]{0,1:T(1,128)}, u32[]{:S(2)}) copy-start(s32[4,1]{0,1:T(1,128)} %param.15) | copy-start | bytes 52
  12.6 7.6 %copy-start.10 = (f32[384,768]{1,0:T(8,128)S(1)}, f32[384,768]{1,0:T(8,128)}, u32[]{:S(2)}) copy-start(f32[384,768]{1,0:T(8,128)} %get-tuple-element.39) | copy-start | bytes 3538948
  12.6 7.6 %copy-start.19 = (pred[192]{0:T(512)(128)(4,1)S(1)}, pred[192]{0:T(512)(128)(4,1)}, u32[]{:S(2)}) copy-start(pred[192]{0:T(512)(128)(4,1)} %iota_compare_fusion.7) | copy-start | bytes 580
  20.3 2.1 %copy-start.15 = (f32[48,768]{1,0:T(8,128)S(1)}, f32[48,768]{1,0:T(8,128)}, u32[]{:S(2)}) copy-start(f32[48,768]{1,0:T(8,128)} %copy-done.14) | copy-start | bytes 442372
  20.4 2.1 %copy-start.17 = (bf16[768]{0:T(1024)(128)(2,1)S(1)}, bf16[768]{0:T(1024)(128)(2,1)}, u32[]{:S(2)}) copy-start(bf16[768]{0:T(1024)(128)(2,1)} %get-tuple-element.44) | copy-start | bytes 4612
  20.4 2.1 %copy-start.18 = (s32[384]{0:T(512)S(1)}, s32[384]{0:T(512)}, u32[]{:S(2)}) copy-start(s32[384]{0:T(512)} %iota_add_fusion) | copy-start | bytes 4612
  20.4 2.1 %copy-start.22 = (bf16[16,48,768]{2,1,0:T(8,128)(2,1)S(1)}, bf16[16,48,768]{2,1,0:T(8,128)(2,1)}, u32[]{:S(2)}) copy-start(bf16[16,48,768]{2,1,0:T(8,128)(2,1)} %param.12) | copy-start | bytes 3538948
  20.4 2.1 %copy-start.24 = (pred[768]{0:T(1024)(128)(4,1)S(1)}, pred[768]{0:T(1024)(128)(4,1)}, u32[]{:S(2)}) copy-start(pred[768]{0:T(1024)(128)(4,1)} %iota_compare_fusion.3) | copy-start | bytes 2308
  20.4 2.1 %copy-start.25 = (pred[384]{0:T(512)(128)(4,1)S(1)}, pred[384]{0:T(512)(128)(4,1)}, u32[]{:S(2)}) copy-start(pred[384]{0:T(512)(128)(4,1)} %get-tuple-element.41) | copy-start | bytes 1156
  20.4 2.1 %copy-start.26 = (pred[384]{0:T(512)(128)(4,1)S(1)}, pred[384]{0:T(512)(128)(4,1)}, u32[]{:S(2)}) copy-start(pred[384]{0:T(512)(128)(4,1)} %get-tuple-element.42) | copy-start | bytes 1156
  22.5 1.1 copy-start.1
  22.5 1.2 copy-start.2
  22.5 1.4 %copy-start.3 = (f32[384,384]{1,0:T(8,128)S(1)}, f32[384,384]{1,0:T(8,128)}, u32[]{:S(2)}) copy-start(f32[384,384]{1,0:T(8,128)} %get-tuple-element.46.refs_1_) | copy-start | bytes 1769476
  22.5 1.4 %copy-start.6 = (f32[384,2]{1,0:T(8,128)S(1)}, f32[384,2]{1,0:T(8,128)}, u32[]{:S(2)}) copy-start(f32[384,2]{1,0:T(8,128)} %get-tuple-element.22.refs_2_) | copy-start | bytes 9220
  22.5 1.6 %copy-start.8 = (bf16[384,768]{1,0:T(8,128)(2,1)S(1)}, bf16[384,768]{1,0:T(8,128)(2,1)}, u32[]{:S(2)}) copy-start(bf16[384,768]{1,0:T(8,128)(2,1)} %constant.85.clone.refs_3_) | copy-start | bytes 1769476
  22.5 1.7 %copy-start.9 = (bf16[384,384]{1,0:T(8,128)(2,1)S(1)}, bf16[384,384]{1,0:T(8,128)(2,1)}, u32[]{:S(2)}) copy-start(bf16[384,384]{1,0:T(8,128)(2,1)} %constant.86.clone.refs_4_) | copy-start | bytes 884740
  24.2 2.3 %copy-start.7 = (bf16[1,8,384,768]{3,2,1,0:T(8,128)(2,1)S(1)}, bf16[1,8,384,768]{3,2,1,0:T(8,128)(2,1)}, u32[]{:S(2)}) copy-start(bf16[1,8,384,768]{3,2,1,0:T(8,128)(2,1)} %param.13) | copy-start | bytes 14155780
  114.4 0.8 copy-start.4
  115.2 5.7 %copy-start.5 = (f32[384,384]{1,0:T(8,128)S(1)}, f32[384,384]{1,0:T(8,128)}, u32[]{:S(2)}) copy-start(f32[384,384]{1,0:T(8,128)} %copy-done.4) | copy-start | bytes 1769476
  116.1 4.8 %collective-permute-start.1 = (bf16[3,192,384]{2,1,0:T(8,128)(2,1)}, bf16[3,192,384]{2,1,0:T(8,128)(2,1)S(1)}, u32[]{:S(2)}, u32[]{:S(2)}) collective-permute-start(bf16[3,192,384]{2,1,0:T(8,128)(2,1)} %pad_maximum_fusion.2), channel_id=1, source_target_pairs={{0,1},{1,0},{2,3},{3,2},{4,5},{5,4},{6,7},{7,6},{8,9},{9,8},{10,11... | collective-permute-start | bytes 1327112 | tf_op jit(solution)/shard_map/ppermute | solution.py:419
  121.1 11.4 %collective-permute-start.2 = (bf16[3,192,384]{2,1,0:T(8,128)(2,1)S(1)}, bf16[3,192,384]{2,1,0:T(8,128)(2,1)S(1)}, u32[]{:S(2)}, u32[]{:S(2)}) collective-permute-start(bf16[3,192,384]{2,1,0:T(8,128)(2,1)S(1)} %pad_maximum_fusion.3), channel_id=1, source_target_pairs={{0,2},{1,3},{2,0},{3,1},{4,6},{5,7},{6,4},{7,5},{8,10},{9,11},{10,... | collective-permute-start | bytes 1327112 | tf_op jit(solution)/shard_map/ppermute | solution.py:423
  132.8 2.7 %collective-permute-start.3 = (bf16[3,192,384]{2,1,0:T(8,128)(2,1)S(1)}, bf16[3,192,384]{2,1,0:T(8,128)(2,1)S(1)}, u32[]{:S(2)}, u32[]{:S(2)}) collective-permute-start(bf16[3,192,384]{2,1,0:T(8,128)(2,1)S(1)} %pad_maximum_fusion.4), channel_id=1, source_target_pairs={{0,1},{1,0},{2,3},{3,2},{4,5},{5,4},{6,7},{7,6},{8,9},{9,8},{10,11... | collective-permute-start | bytes 1327112 | tf_op jit(solution)/shard_map/ppermute | solution.py:426
